TPU v7x, 512 devices: a whole 4x8x8 slice. The times are simulated.
512 devices in a mesh: inst: 64 (over z_hi, x, y), tp: 8 (over z_lo, core).
Axes of the slice: x: 4, y: 8, z: 8 (z_hi: 2, z_lo: 4; z = z_hi * 4 + z_lo), core: 2. Of those that a mesh axis runs over, the one named last changes fastest.
Arguments:
- step_queries: bfloat16 [4, 512, 8192], P(None, 'inst', 'tp'), may hold values from -11 to 11
- step_keyvals: bfloat16 [4, 512, 8, 256], P(None, 'inst', 'tp'), may hold values from -9.5 to 9.5
- cache_pages: bfloat16 [8192, 16, 8, 256], P('inst', None, 'tp'), may hold values from -9.5 to 9.5
- block_table: int32 [512, 16], P('inst'), may hold values from 0 to 127, as said below
- context_len: int32 [512], replicated, may hold values from 1 to 256, as said below
- partner: int32 [64], replicated, may hold values from 0 to 63, as said below
- moved_slot: int32 [64], replicated, may hold values from 0 to 7
- prompt_queries: bfloat16 [32768, 8192], P(('inst', 'tp')), may hold values from -11 to 11
- prompt_keyvals: bfloat16 [32768, 8, 256], P(('inst', 'tp')), may hold values from -9.5 to 9.5
- prompt_target: int32 [32768, 1], replicated, may hold values from 0 to 63; in each aligned block of 64 rows (0 to 63, 64 to 127, ...) at most 2 rows name the same one
Outputs:
- decode_output: bfloat16 [4, 512, 8192], P(None, 'inst', 'tp')
- prefill_output: bfloat16 [65536, 8192], P('inst', 'tp')
Inputs may be any that keep to these rules, and one draw needn't show every extreme that they name: partner[partner[i]] = i, and i and partner[i] differ in exactly one bit. `block_table`: the 8 rows of one instance together name each of its 128 pages once. `context_len`: some request holds exactly 256 tokens. `prompt_target`: among the 64 rows of one device no instance is named more than 2 times.
All inputs are finite; a program needn't handle non-finite values.
Results may differ from a plain program's by a relative error of at most 0.0049.
Values may be sent and summed in bfloat16 or wider, within the bound.
No kernel may reach another device: no remote copies, remote signals or barrier semaphores. Data moves between devices by JAX's collectives and lax.ppermute only.
A program may use at most 64 MiB of HBM per device.

v0:
```python
import jax
import jax.numpy as jnp
from jax import lax
from jax.sharding import PartitionSpec as P


def swapped(array, axis, bit):
    return lax.ppermute(array, axis, [(i, i ^ 1 << bit) for i in range(lax.axis_size(axis))])


def masked_weights(scores, mask):
    shifted = jnp.where(mask, scores, jnp.float32(-1e30))
    top = jnp.max(shifted, axis=-1, keepdims=True)
    expo = jnp.where(mask, jnp.exp(shifted - top), jnp.float32(0.0))
    total = jnp.sum(expo, axis=-1, keepdims=True)
    total = jnp.where(total > 0, total, jnp.float32(1.0))
    return expo / total


def decode_block(queries, context, lengths, fresh):
    steps, count, width = queries.shape
    kv_heads = context.shape[2]
    head_dim = context.shape[3] // 2
    group = width // (kv_heads * head_dim)
    span = context.shape[1]
    scale = head_dim ** (-0.5)
    query = queries.reshape(steps, count, kv_heads, group, head_dim)
    past = (
        jnp.einsum(
            "trkgd,rckd->trkgc", query, context[..., :head_dim], preferred_element_type=jnp.float32
        )
        * scale
    )
    newer = (
        jnp.einsum(
            "trkgd,urkd->trkgu", query, fresh[..., :head_dim], preferred_element_type=jnp.float32
        )
        * scale
    )
    past_mask = (jnp.arange(span, dtype=jnp.int32)[None, :] < lengths[:, None])[
        None, :, None, None, :
    ]
    step_ids = jnp.arange(steps, dtype=jnp.int32)
    new_mask = (step_ids[None, :] <= step_ids[:, None])[:, None, None, None, :]
    mask = jnp.concatenate(
        [jnp.broadcast_to(past_mask, past.shape), jnp.broadcast_to(new_mask, newer.shape)], axis=-1
    )
    weights = masked_weights(jnp.concatenate([past, newer], axis=-1), mask).astype(jnp.bfloat16)
    out = jnp.einsum(
        "trkgc,rckd->trkgd",
        weights[..., :span],
        context[..., head_dim:],
        preferred_element_type=jnp.float32,
    )
    out = out + jnp.einsum(
        "trkgu,urkd->trkgd",
        weights[..., span:],
        fresh[..., head_dim:],
        preferred_element_type=jnp.float32,
    )
    return out.reshape(steps, count, width).astype(jnp.bfloat16)


def prefill_block(queries, keyvals, valid):
    slots, width = queries.shape
    kv_heads = keyvals.shape[1]
    head_dim = keyvals.shape[2] // 2
    group = width // (kv_heads * head_dim)
    scale = head_dim ** (-0.5)
    query = queries.reshape(slots, kv_heads, group, head_dim)
    block = 512
    pieces = []
    for start in range(0, slots, block):
        finish = start + block
        scores = (
            jnp.einsum(
                "qkgd,ckd->kgqc",
                query[start:finish],
                keyvals[:finish, :, :head_dim],
                preferred_element_type=jnp.float32,
            )
            * scale
        )
        query_pos = jnp.arange(start, finish, dtype=jnp.int32)
        key_pos = jnp.arange(finish, dtype=jnp.int32)
        mask = (valid[None, :finish] & (key_pos[None, :] <= query_pos[:, None]))[None, None]
        weights = masked_weights(scores, jnp.broadcast_to(mask, scores.shape)).astype(jnp.bfloat16)
        out = jnp.einsum(
            "kgqc,ckd->qkgd",
            weights,
            keyvals[:finish, :, head_dim:],
            preferred_element_type=jnp.float32,
        )
        out = jnp.where(valid[start:finish, None, None, None], out, jnp.float32(0.0))
        pieces.append(out.reshape(block, width).astype(jnp.bfloat16))
    return jnp.concatenate(pieces, axis=0)


def local(
    step_queries,
    step_keyvals,
    cache_pages,
    block_table,
    context_len,
    partner,
    moved_slot,
    prompt_queries,
    prompt_keyvals,
    prompt_target,
):
    inst_count = lax.axis_size("inst")
    tp_count = lax.axis_size("tp")
    me_inst = lax.axis_index("inst")
    me_tp = lax.axis_index("tp")
    requests = block_table.shape[0]
    kv_heads = step_keyvals.shape[2]
    head_dim = step_keyvals.shape[3] // 2
    rows_dev = prompt_queries.shape[0]
    capacity = max(2, 2 * rows_dev // inst_count)
    devices = inst_count * tp_count
    targets = prompt_target[:, 0].reshape(devices, rows_dev)
    mine = lax.dynamic_index_in_dim(targets, me_inst * tp_count + me_tp, 0, keepdims=False)
    onehot = (mine[:, None] == jnp.arange(inst_count, dtype=jnp.int32)[None, :]).astype(jnp.int32)
    rank = jnp.sum((jnp.cumsum(onehot, axis=0) - onehot) * onehot, axis=1)
    place = mine * capacity + rank
    dispatch = (
        jnp.arange(inst_count * capacity, dtype=jnp.int32)[:, None] == place[None, :]
    ).astype(jnp.bfloat16)
    send_queries = (
        jnp.dot(dispatch, prompt_queries, preferred_element_type=jnp.float32)
        .astype(jnp.bfloat16)
        .reshape(inst_count, capacity, -1)
    )
    flat_keyvals = prompt_keyvals.reshape(rows_dev, -1)
    send_keyvals = (
        jnp.dot(dispatch, flat_keyvals, preferred_element_type=jnp.float32)
        .astype(jnp.bfloat16)
        .reshape(inst_count, capacity, -1)
    )
    recv_queries, recv_keyvals = (
        lax.all_to_all(
            lax.all_to_all(send_queries, "inst", split_axis=0, concat_axis=0, tiled=True),
            "tp",
            split_axis=2,
            concat_axis=1,
            tiled=True,
        ),
        lax.all_to_all(
            lax.all_to_all(send_keyvals, "inst", split_axis=0, concat_axis=0, tiled=True),
            "tp",
            split_axis=2,
            concat_axis=1,
            tiled=True,
        ),
    )
    gathered = cache_pages[block_table]
    context = gathered.reshape(requests, -1, kv_heads, 2 * head_dim)
    lengths = lax.dynamic_slice_in_dim(context_len, me_inst * requests, requests)
    my_slot = moved_slot[me_inst]
    other = partner[me_inst]
    other_len = context_len[other * requests + moved_slot[other]]
    bit_total = inst_count.bit_length() - 1
    distance = jnp.bitwise_xor(me_inst, other)
    outgoing = lax.dynamic_index_in_dim(context, my_slot, 0, keepdims=False)
    incoming = outgoing
    for bit in range(bit_total):
        arrived = swapped(outgoing, "inst", bit)
        incoming = jnp.where(distance == 1 << bit, arrived, incoming)
    context = lax.dynamic_update_index_in_dim(context, incoming, my_slot, 0)
    lengths = lengths.at[my_slot].set(other_len)
    decode_output = decode_block(step_queries, context, lengths, step_keyvals)
    slots = inst_count * tp_count * capacity
    slot_queries = recv_queries.reshape(slots, -1)
    slot_keyvals = recv_keyvals.reshape(slots, kv_heads, 2 * head_dim)
    counts = jnp.sum((targets == me_inst).astype(jnp.int32), axis=1)
    valid = (jnp.arange(capacity, dtype=jnp.int32)[None, :] < counts[:, None]).reshape(slots)
    prefill_output = prefill_block(slot_queries, slot_keyvals, valid)
    return (decode_output, prefill_output)


def solution(mesh):
    placed = (
        P(None, "inst", "tp"),
        P(None, "inst", "tp", None),
        P("inst", None, "tp", None),
        P("inst", None),
        P(),
        P(),
        P(),
        P(("inst", "tp"), None),
        P(("inst", "tp"), None, None),
        P(),
    )
    return jax.shard_map(
        local,
        mesh=mesh,
        in_specs=placed,
        out_specs=(P(None, "inst", "tp"), P("inst", "tp")),
        check_vma=False,
    )
```

profile of v0, /device:TPU:1, one launch (start us, length us, event | category | flops | bytes accessed | tf_op | source)
XLA Modules:
  0.0 244.2 jit_solution(7322671740194920094)
XLA Ops:
  0.7 0.5 broadcast.263
  1.2 1.9 reduce.11
  3.5 1.0 copy.94
  4.5 0.3 convolution_convert_fusion.1
  4.8 1.1 reshape.492
  6.0 20.0 %all-to-all-start = ((bf16[64,2,2048]{2,1,0:T(2,128)(2,1)}), bf16[64,2,2048]{2,1,0:T(2,128)(2,1)}, u32[]{:S(2)}, u32[]{:S(2)}) async-start(bf16[64,2,2048]{2,1,0:T(2,128)(2,1)} %reshape.492), calls=%async_computation | async-start | bytes 1048576 | tf_op jit(solution)/shard_map/all_to_all | solution.py:149
  25.9 0.7 convolution_convert_fusion
  26.6 2.6 %reshape.496 = bf16[64,2,8192]{2,1,0:T(2,128)(2,1)} reshape(bf16[128,8192]{1,0:T(8,128)(2,1)S(1)} %convolution_convert_fusion) | data formatting | bytes 4194304 | tf_op jit(solution)/shard_map/reshape | solution.py:132
  29.3 17.0 %all-to-all-done = bf16[64,2,2048]{2,1,0:T(2,128)(2,1)} async-done(((bf16[64,2,2048]{2,1,0:T(2,128)(2,1)}), bf16[64,2,2048]{2,1,0:T(2,128)(2,1)}, u32[]{:S(2)}, u32[]{:S(2)}) %all-to-all-start) | async-done | bytes 524320 | tf_op jit(solution)/shard_map/all_to_all | solution.py:149
  46.2 6.5 %all-to-all-start.2 = ((bf16[64,2,8192]{2,1,0:T(2,128)(2,1)}), bf16[64,2,8192]{2,1,0:T(2,128)(2,1)S(1)}, u32[]{:S(2)}, u32[]{:S(2)}) async-start(bf16[64,2,8192]{2,1,0:T(2,128)(2,1)} %reshape.496), calls=%async_computation.2 | async-start | bytes 4194304 | tf_op jit(solution)/shard_map/all_to_all | solution.py:142
  52.7 2.6 %copy.67 = bf16[64,2,2048]{0,1,2:T(2,128)(2,1)S(1)} copy(bf16[64,2,2048]{2,1,0:T(2,128)(2,1)} %all-to-all-done) | data formatting | bytes 1048576 | tf_op jit(solution)/shard_map/all_to_all | solution.py:149
  55.3 1.5 reshape.536
  56.8 48.4 %all-to-all-done.2 = bf16[64,2,8192]{2,1,0:T(2,128)(2,1)S(1)} async-done(((bf16[64,2,8192]{2,1,0:T(2,128)(2,1)}), bf16[64,2,8192]{2,1,0:T(2,128)(2,1)S(1)}, u32[]{:S(2)}, u32[]{:S(2)}) %all-to-all-start.2) | async-done | bytes 2097184 | tf_op jit(solution)/shard_map/all_to_all | solution.py:142
  105.3 7.9 %all-to-all-start.1 = ((bf16[8,2,16384]{2,1,0:T(2,128)(2,1)}), bf16[8,2,16384]{2,1,0:T(2,128)(2,1)S(1)}, u32[]{:S(2)}, u32[]{:S(2)}) async-start(bf16[8,2,16384]{2,1,0:T(2,128)(2,1)} %reshape.536), calls=%async_computation.1 | async-start | bytes 1048576 | tf_op jit(solution)/shard_map/all_to_all | solution.py:148
  113.1 0.6 dynamic_slice.25
  115.7 0.7 fusion.43
  117.6 7.7 %copy.69 = bf16[64,2,8192]{0,1,2:T(2,128)(2,1)} copy(bf16[64,2,8192]{2,1,0:T(2,128)(2,1)S(1)} %all-to-all-done.2) | data formatting | bytes 4194304 | tf_op jit(solution)/shard_map/all_to_all | solution.py:142
  125.3 7.6 %reshape.534 = bf16[8,2,65536]{2,1,0:T(2,128)(2,1)} reshape(bf16[8192,2,64]{2,1,0:T(2,128)(2,1)} %bitcast.160) | data formatting | bytes 4194304
  132.9 5.1 %all-to-all-start.3 = ((bf16[8,2,65536]{2,1,0:T(2,128)(2,1)}), bf16[8,2,65536]{2,1,0:T(2,128)(2,1)}, u32[]{:S(2)}, u32[]{:S(2)}) async-start(bf16[8,2,65536]{2,1,0:T(2,128)(2,1)} %reshape.534), calls=%async_computation.3 | async-start | bytes 4194304 | tf_op jit(solution)/shard_map/all_to_all | solution.py:141
  138.8 1.9 gather_fusion
  140.7 3.7 %collective-permute-start = (bf16[256,1,256]{2,0,1:T(8,128)(2,1)S(1)}, bf16[256,1,256]{2,0,1:T(8,128)(2,1)S(1)}, u32[]{:S(2)}, u32[]{:S(2)}) collective-permute-start(bf16[256,1,256]{2,0,1:T(8,128)(2,1)S(1)} %dynamic-slice_bitcast_fusion), channel_id=1, source_target_pairs={{0,256},{8,264},{16,272},{24,280},{32,288},{40,296},{48,304},{56,3... | collective-permute-start | bytes 393224 | tf_op jit(solution)/shard_map/ppermute | solution.py:8
  144.4 3.3 %collective-permute-start.1 = (bf16[256,1,256]{2,0,1:T(8,128)(2,1)S(1)}, bf16[256,1,256]{2,0,1:T(8,128)(2,1)S(1)}, u32[]{:S(2)}, u32[]{:S(2)}) collective-permute-start(bf16[256,1,256]{2,0,1:T(8,128)(2,1)S(1)} %dynamic-slice_bitcast_fusion), channel_id=1, source_target_pairs={{0,128},{8,136},{16,144},{24,152},{32,160},{40,168},{48,176},{56,1... | collective-permute-start | bytes 393224 | tf_op jit(solution)/shard_map/ppermute | solution.py:8
  147.7 1.9 collective-permute-start.2
  149.7 3.7 %collective-permute-start.3 = (bf16[256,1,256]{2,0,1:T(8,128)(2,1)S(1)}, bf16[256,1,256]{2,0,1:T(8,128)(2,1)S(1)}, u32[]{:S(2)}, u32[]{:S(2)}) collective-permute-start(bf16[256,1,256]{2,0,1:T(8,128)(2,1)S(1)} %dynamic-slice_bitcast_fusion), channel_id=1, source_target_pairs={{0,32},{8,40},{16,48},{24,56},{32,0},{40,8},{48,16},{56,24},{64,96... | collective-permute-start | bytes 393224 | tf_op jit(solution)/shard_map/ppermute | solution.py:8
  153.3 4.0 %collective-permute-start.4 = (bf16[256,1,256]{2,0,1:T(8,128)(2,1)S(1)}, bf16[256,1,256]{2,0,1:T(8,128)(2,1)}, u32[]{:S(2)}, u32[]{:S(2)}) collective-permute-start(bf16[256,1,256]{2,0,1:T(8,128)(2,1)S(1)} %dynamic-slice_bitcast_fusion), channel_id=1, source_target_pairs={{0,16},{8,24},{16,0},{24,8},{32,48},{40,56},{48,32},{56,40},{64,80... | collective-permute-start | bytes 393224 | tf_op jit(solution)/shard_map/ppermute | solution.py:8
  159.7 0.4 fusion.11
  160.2 20.3 %collective-permute-done = bf16[256,1,256]{2,0,1:T(8,128)(2,1)S(1)} collective-permute-done((bf16[256,1,256]{2,0,1:T(8,128)(2,1)S(1)}, bf16[256,1,256]{2,0,1:T(8,128)(2,1)S(1)}, u32[]{:S(2)}, u32[]{:S(2)}) %collective-permute-start) | collective-permute-done | bytes 131104 | tf_op jit(solution)/shard_map/ppermute | solution.py:8
  180.5 3.6 %collective-permute-start.5 = (bf16[256,1,256]{2,0,1:T(8,128)(2,1)S(1)}, bf16[256,1,256]{2,0,1:T(8,128)(2,1)S(1)}, u32[]{:S(2)}, u32[]{:S(2)}) collective-permute-start(bf16[256,1,256]{2,0,1:T(8,128)(2,1)S(1)} %dynamic-slice_bitcast_fusion), channel_id=1, source_target_pairs={{0,8},{8,0},{16,24},{24,16},{32,40},{40,32},{48,56},{56,48},{64,72... | collective-permute-start | bytes 393224 | tf_op jit(solution)/shard_map/ppermute | solution.py:8
  185.1 2.3 collective-permute-done.5
  187.6 0.3 fusion.16
  188.1 0.3 fusion.25
  188.9 0.7 copy.79
  189.6 3.0 %reshape.537 = bf16[2048,2,64]{2,1,0:T(2,128)(2,1)S(1)} reshape(bf16[8,2,16384]{2,1,0:T(2,128)(2,1)} %copy-done.2) | data formatting | bytes 1048576
  192.6 0.8 copy.68
  193.6 7.4 %reshape.535 = bf16[8192,2,64]{2,1,0:T(2,128)(2,1)} reshape(bf16[8,2,65536]{2,1,0:T(2,128)(2,1)} %all-to-all-done.3) | data formatting | bytes 4194304
  201.0 11.1 %copy.70 = bf16[64,2,8,1024]{3,1,2,0:T(2,128)(2,1)} copy(bf16[64,2,8,1024]{0,1,3,2:T(2,128)(2,1)} %bitcast.161) | data formatting | bytes 4194304 | tf_op jit(solution)/shard_map/all_to_all | solution.py:141
  212.1 4.0 %fusion.40 = (bf16[32,8,2,1024]{3,2,1,0:T(2,128)(2,1)S(1)}, bf16[32,8,2,1024]{3,2,1,0:T(2,128)(2,1)}) fusion(bf16[64,8,2,1024]{3,2,1,0:T(2,128)(2,1)} %bitcast.162), kind=kLoop, calls=%fused_computation.86 | loop fusion | bytes 4194304 | tf_op jit(solution)/shard_map/slice | solution.py:78
  216.1 0.7 reshape.497
  216.8 1.6 fusion.4
  218.5 2.0 fusion.5
  220.5 2.9 %fusion.10 = bf16[1,128,8,512]{3,1,2,0:T(8,128)(2,1)S(1)} fusion(f32[8,512]{1,0:T(8,128)S(1)} %compare_select_fusion.1, f32[8,512]{1,0:T(8,128)S(1)} %get-tuple-element.32, f32[512,512,8]{1,0,2:T(8,128)S(1)} %get-tuple-element.33, pred[512,512]{0,1:T(8,128)(4,1)S(1)} %fusion.24, pred[512]{0:T(512)(128)(4,1)S(1)} %copy-done.7, ...), kind=kOutput, calls=%fused_computation.22 | convolution fusion | flops 550502400 | bytes 9863680 | tf_op jit(solution)/shard_map/kgqc,ckd->qkgd/dot_general | solution.py:88
  223.4 0.5 copy.77
  224.0 1.7 reshape.501
  225.7 3.0 %fusion = (f32[8,512]{1,0:T(8,128)S(1)}, f32[1024,512,8]{1,0,2:T(8,128)S(1)}) fusion(pred[512,1024]{0,1:T(8,128)(4,1)S(1)} %fusion.11, bf16[512,8,128]{2,1,0:T(8,128)(2,1)S(1)} %reshape.501, bf16[1024,1,256]{2,0,1:T(8,128)(2,1)S(1)} %reshape.493), kind=kOutput, calls=%fused_computation.4 | convolution fusion | flops 1086320640 | bytes 18628608 | tf_op jit(solution)/shard_map/qkgd,ckd->kgqc/dot_general | solution.py:76
  228.7 4.2 %fusion.1 = f32[8,512]{1,0:T(8,128)S(1)} fusion(f32[1024,512,8]{1,0,2:T(8,128)S(1)} %get-tuple-element.31, f32[8,512]{1,0:T(8,128)S(1)} %get-tuple-element.30, pred[512,1024]{0,1:T(8,128)(4,1)S(1)} %fusion.11), kind=kLoop, calls=%fused_computation.5 | loop fusion | flops 20967424 | bytes 17334272 | tf_op jit(solution)/shard_map/reduce_sum | solution.py:15
  233.0 6.3 %fusion.9 = bf16[1,128,8,512]{3,1,2,0:T(8,128)(2,1)} fusion(f32[8,512]{1,0:T(8,128)S(1)} %compare_select_fusion, f32[8,512]{1,0:T(8,128)S(1)} %get-tuple-element.30, f32[1024,512,8]{1,0,2:T(8,128)S(1)} %get-tuple-element.31, pred[512,1024]{0,1:T(8,128)(4,1)S(1)} %fusion.11, pred[512]{0:T(512)(128)(4,1)S(1)} %broadcast_in_dim.121, ...), kind=kOutput, calls=%fused_computation.20 | convolution fusion | flops 1099956224 | bytes 18645504 | tf_op jit(solution)/shard_map/kgqc,ckd->qkgd/dot_general | solution.py:88
  239.3 2.3 copy.78
  241.5 2.7 %pad_maximum_fusion = bf16[1024,1024]{1,0:T(8,128)(2,1)} fusion(bf16[512,1024]{1,0:T(8,128)(2,1)} %copy.78, bf16[512,1024]{1,0:T(8,128)(2,1)S(1)} %copy.77), kind=kLoop, calls=%fused_computation.18 | loop fusion | flops 4194304 | bytes 4194304 | tf_op jit(solution)/shard_map/concatenate | solution.py:96
  (64 shorter events, 3.1 us)
Async XLA Ops:
  0.6 25.3 %copy-start = (bf16[64,8192]{1,0:T(8,128)(2,1)S(1)}, bf16[64,8192]{1,0:T(8,128)(2,1)}, u32[]{:S(2)}) copy-start(bf16[64,8192]{1,0:T(8,128)(2,1)} %param.19) | copy-start | bytes 3145732
  6.0 107.2 %copy-start.10 = (s32[64]{0:T(128)S(1)}, s32[64]{0:T(128)}, u32[]{:S(2)}) copy-start(s32[64]{0:T(128)} %param.17) | copy-start | bytes 772
  6.0 109.7 %copy-start.8 = (s32[64]{0:T(128)S(1)}, s32[64]{0:T(128)}, u32[]{:S(2)}) copy-start(s32[64]{0:T(128)} %param.18) | copy-start | bytes 772
  6.0 40.3 %all-to-all-start = ((bf16[64,2,2048]{2,1,0:T(2,128)(2,1)}), bf16[64,2,2048]{2,1,0:T(2,128)(2,1)}, u32[]{:S(2)}, u32[]{:S(2)}) async-start(bf16[64,2,2048]{2,1,0:T(2,128)(2,1)} %reshape.492), calls=%async_computation | async-start | bytes 1048576 | tf_op jit(solution)/shard_map/all_to_all | solution.py:149
  46.2 59.0 %all-to-all-start.2 = ((bf16[64,2,8192]{2,1,0:T(2,128)(2,1)}), bf16[64,2,8192]{2,1,0:T(2,128)(2,1)S(1)}, u32[]{:S(2)}, u32[]{:S(2)}) async-start(bf16[64,2,8192]{2,1,0:T(2,128)(2,1)} %reshape.496), calls=%async_computation.2 | async-start | bytes 4194304 | tf_op jit(solution)/shard_map/all_to_all | solution.py:142
  105.3 27.7 %all-to-all-start.1 = ((bf16[8,2,16384]{2,1,0:T(2,128)(2,1)}), bf16[8,2,16384]{2,1,0:T(2,128)(2,1)S(1)}, u32[]{:S(2)}, u32[]{:S(2)}) async-start(bf16[8,2,16384]{2,1,0:T(2,128)(2,1)} %reshape.536), calls=%async_computation.1 | async-start | bytes 1048576 | tf_op jit(solution)/shard_map/all_to_all | solution.py:148
  117.6 20.4 %copy-start.5 = (s32[8,16]{1,0:T(8,128)S(1)}, s32[8,16]{1,0:T(8,128)}, u32[]{:S(2)}) copy-start(s32[8,16]{1,0:T(8,128)} %param.15) | copy-start | bytes 1540
  117.6 42.0 %copy-start.4 = (bf16[4,8,1,256]{3,1,2,0:T(8,128)(2,1)S(1)}, bf16[4,8,1,256]{3,1,2,0:T(8,128)(2,1)}, u32[]{:S(2)}) copy-start(bf16[4,8,1,256]{3,1,2,0:T(8,128)(2,1)} %param.13) | copy-start | bytes 49156
  125.3 34.0 %copy-start.9 = (s32[512]{0:T(512)S(1)}, s32[512]{0:T(512)}, u32[]{:S(2)}) copy-start(s32[512]{0:T(512)} %param.16) | copy-start | bytes 6148
  125.3 59.6 %copy-start.3 = (bf16[4,8,1024]{2,1,0:T(8,128)(2,1)S(1)}, bf16[4,8,1024]{2,1,0:T(8,128)(2,1)}, u32[]{:S(2)}) copy-start(bf16[4,8,1024]{2,1,0:T(8,128)(2,1)} %param.12) | copy-start | bytes 196612
  132.9 54.5 %copy-start.2 = (bf16[8,2,16384]{2,1,0:T(2,128)(2,1)}, bf16[8,2,16384]{2,1,0:T(2,128)(2,1)S(1)}, u32[]{:S(2)}) copy-start(bf16[8,2,16384]{2,1,0:T(2,128)(2,1)S(1)} %all-to-all-done.1) | copy-start | bytes 1572868
  132.9 60.6 %all-to-all-start.3 = ((bf16[8,2,65536]{2,1,0:T(2,128)(2,1)}), bf16[8,2,65536]{2,1,0:T(2,128)(2,1)}, u32[]{:S(2)}, u32[]{:S(2)}) async-start(bf16[8,2,65536]{2,1,0:T(2,128)(2,1)} %reshape.534), calls=%async_computation.3 | async-start | bytes 4194304 | tf_op jit(solution)/shard_map/all_to_all | solution.py:141
  140.7 39.8 %collective-permute-start = (bf16[256,1,256]{2,0,1:T(8,128)(2,1)S(1)}, bf16[256,1,256]{2,0,1:T(8,128)(2,1)S(1)}, u32[]{:S(2)}, u32[]{:S(2)}) collective-permute-start(bf16[256,1,256]{2,0,1:T(8,128)(2,1)S(1)} %dynamic-slice_bitcast_fusion), channel_id=1, source_target_pairs={{0,256},{8,264},{16,272},{24,280},{32,288},{40,296},{48,304},{56,3... | collective-permute-start | bytes 393224 | tf_op jit(solution)/shard_map/ppermute | solution.py:8
  144.4 40.7 %collective-permute-start.1 = (bf16[256,1,256]{2,0,1:T(8,128)(2,1)S(1)}, bf16[256,1,256]{2,0,1:T(8,128)(2,1)S(1)}, u32[]{:S(2)}, u32[]{:S(2)}) collective-permute-start(bf16[256,1,256]{2,0,1:T(8,128)(2,1)S(1)} %dynamic-slice_bitcast_fusion), channel_id=1, source_target_pairs={{0,128},{8,136},{16,144},{24,152},{32,160},{40,168},{48,176},{56,1... | collective-permute-start | bytes 393224 | tf_op jit(solution)/shard_map/ppermute | solution.py:8
  147.7 37.3 %collective-permute-start.2 = (bf16[256,1,256]{2,0,1:T(8,128)(2,1)S(1)}, bf16[256,1,256]{2,0,1:T(8,128)(2,1)S(1)}, u32[]{:S(2)}, u32[]{:S(2)}) collective-permute-start(bf16[256,1,256]{2,0,1:T(8,128)(2,1)S(1)} %dynamic-slice_bitcast_fusion), channel_id=1, source_target_pairs={{0,64},{8,72},{16,80},{24,88},{32,96},{40,104},{48,112},{56,120},{... | collective-permute-start | bytes 393224 | tf_op jit(solution)/shard_map/ppermute | solution.py:8
  149.7 35.4 %collective-permute-start.3 = (bf16[256,1,256]{2,0,1:T(8,128)(2,1)S(1)}, bf16[256,1,256]{2,0,1:T(8,128)(2,1)S(1)}, u32[]{:S(2)}, u32[]{:S(2)}) collective-permute-start(bf16[256,1,256]{2,0,1:T(8,128)(2,1)S(1)} %dynamic-slice_bitcast_fusion), channel_id=1, source_target_pairs={{0,32},{8,40},{16,48},{24,56},{32,0},{40,8},{48,16},{56,24},{64,96... | collective-permute-start | bytes 393224 | tf_op jit(solution)/shard_map/ppermute | solution.py:8
  153.3 31.8 %collective-permute-start.4 = (bf16[256,1,256]{2,0,1:T(8,128)(2,1)S(1)}, bf16[256,1,256]{2,0,1:T(8,128)(2,1)}, u32[]{:S(2)}, u32[]{:S(2)}) collective-permute-start(bf16[256,1,256]{2,0,1:T(8,128)(2,1)S(1)} %dynamic-slice_bitcast_fusion), channel_id=1, source_target_pairs={{0,16},{8,24},{16,0},{24,8},{32,48},{40,56},{48,32},{56,40},{64,80... | collective-permute-start | bytes 393224 | tf_op jit(solution)/shard_map/ppermute | solution.py:8
  159.3 25.6 %copy-start.6 = (pred[512]{0:T(512)(128)(4,1)}, pred[512]{0:T(512)(128)(4,1)S(1)}, u32[]{:S(2)}) copy-start(pred[512]{0:T(512)(128)(4,1)S(1)} %broadcast_in_dim.114) | copy-start | bytes 1540
  180.5 7.0 %collective-permute-start.5 = (bf16[256,1,256]{2,0,1:T(8,128)(2,1)S(1)}, bf16[256,1,256]{2,0,1:T(8,128)(2,1)S(1)}, u32[]{:S(2)}, u32[]{:S(2)}) collective-permute-start(bf16[256,1,256]{2,0,1:T(8,128)(2,1)S(1)} %dynamic-slice_bitcast_fusion), channel_id=1, source_target_pairs={{0,8},{8,0},{16,24},{24,16},{32,40},{40,32},{48,56},{56,48},{64,72... | collective-permute-start | bytes 393224 | tf_op jit(solution)/shard_map/ppermute | solution.py:8
  216.8 3.7 %copy-start.7 = (pred[512]{0:T(512)(128)(4,1)S(1)}, pred[512]{0:T(512)(128)(4,1)}, u32[]{:S(2)}) copy-start(pred[512]{0:T(512)(128)(4,1)} %copy-done.6) | copy-start | bytes 1540
  233.0 11.2 %copy-start.1 = (bf16[64,8192]{1,0:T(8,128)(2,1)S(1)}, bf16[64,8192]{1,0:T(8,128)(2,1)}, u32[]{:S(2)}) copy-start(bf16[64,8192]{1,0:T(8,128)(2,1)} %param.19) | copy-start | bytes 3145732
where the time goes:
time: 246 us; the launch traced here: 244 us
  waiting for transfers between devices  88 us (36%)
  local copies, waits for them, and re-layouts  61.1 us (25%)
  starting transfers between devices  59.7 us (24%)
  matrix products  15.5 us (6%)
  other arithmetic  13 us (5%)
  between operations  6.95 us (3%)
    all_to_all x1, waiting for transfers between devices, local(): lax.all_to_all(send_queries, 'inst', split_axis=0, concat_axis=0, tiled=T...  48.4 us
    ppermute x6, waiting for transfers between devices, swapped(): lax.ppermute(array, axis, [(i, i ^ 1 << bit) for i in range(lax.axis_size...  22.6 us
    unnamed x29, local copies, waits for them, and re-layouts  21.7 us
    ppermute x6, starting transfers between devices, swapped(): lax.ppermute(array, axis, [(i, i ^ 1 << bit) for i in range(lax.axis_size...  20.2 us
    all_to_all x1, starting transfers between devices, local(): lax.all_to_all(send_keyvals, 'inst', split_axis=0, concat_axis=0, tiled=T...  20 us
    all_to_all x1, waiting for transfers between devices, local(): lax.all_to_all(send_keyvals, 'inst', split_axis=0, concat_axis=0, tiled=T...  17 us
    all_to_all x1, local copies, waits for them, and re-layouts, local(): lax.all_to_all(lax.all_to_all(send_queries, 'inst', split_axis=0, concat_...  11.1 us
    dot_general x2, matrix products, prefill_block(): jnp.einsum('kgqc,ckd->qkgd', weights, keyvals[:finish, :, head_dim:], pre...  9.18 us
  transfers between devices with their start and end apart: 10, of which 4 were waited for; matrix products, arithmetic and copies ran while one was open for 14% of the time, Pallas kernels for 0%

commit v1 on v0

v1 whole, which is shorter than its diff:
```python
import functools
import math

import jax
import jax.numpy as jnp
from jax import lax
from jax.experimental import pallas as pl
from jax.experimental.pallas import tpu as pltpu
from jax.sharding import PartitionSpec as P

H, KVH, HD = 64, 8, 128
REQ, PAGE, MAXP, STEPS = 8, 16, 16, 4
ROWS_DEV, CTX, POOL, CAP, SLOTS = 64, 256, 128, 2, 1024
N_INST, N_TP = 64, 8
GROUP = H // KVH
TILES = GROUP + 2
MESSAGE = TILES * CAP
LANES = 128
LOG2_SCALE = HD**-0.5 * math.log2(math.e)
MASKED = -1e30
VMEM = 48 * 1024 * 1024


def iota(shape, dim):
    return lax.broadcasted_iota(jnp.int32, shape, dim)


def dot(a, b, contract=((1,), (0,))):
    return lax.dot_general(a, b, (contract, ((), ())), preferred_element_type=jnp.float32)


NT = ((1,), (1,))


INSTS = 8


def dispatch_kernel(me_ref, target_ref, queries_ref, keyvals_ref, out_ref, place_ref, rows_ref):
    step = pl.program_id(0)

    @pl.when(step == 0)
    def _():
        me = me_ref[0]
        line = lax.rem(lax.div(me, 2), 8)
        both = jnp.sum(
            jnp.where(iota((8, LANES), 0) == line, target_ref[...], 0), axis=0, keepdims=True
        )
        both = jnp.broadcast_to(both, (8, LANES))
        other = pltpu.roll(both, ROWS_DEV, 1)
        first = iota((8, LANES), 1) < ROWS_DEV
        odd = lax.rem(me, 2) == 1
        mine = jnp.where(first != odd, both, other)[0:1]
        down, along = iota((ROWS_DEV, LANES), 0), iota((ROWS_DEV, LANES), 1)
        wide = jnp.broadcast_to(mine, (ROWS_DEV, LANES))
        column = jnp.sum(jnp.where(down == along, wide, 0), axis=1, keepdims=True)
        earlier = (column == wide) & (down < along % ROWS_DEV)
        rank = jnp.sum(earlier.astype(jnp.int32), axis=0, keepdims=True)
        place = jnp.broadcast_to(mine * CAP + rank, (8, LANES))
        for i in range(4):
            place_ref[:, i * LANES : (i + 1) * LANES] = place
        down, along = iota((512, 512), 0), iota((512, 512), 1)
        order = (down % ROWS_DEV == along // KVH) & (down // ROWS_DEV == along % KVH)
        keyvals = dot(order.astype(jnp.float32).astype(jnp.bfloat16), keyvals_ref[...])
        keyvals = keyvals.astype(jnp.bfloat16)
        for c in range(N_TP * TILES):
            tp, tile = divmod(c, TILES)
            if tile < GROUP:
                piece = queries_ref[:, (tp * GROUP + tile) * HD : (tp * GROUP + tile + 1) * HD]
            else:
                lane = (tile - GROUP) * HD
                piece = keyvals[tp * ROWS_DEV : (tp + 1) * ROWS_DEV, lane : lane + HD]
            to, col = c % 8, c // 8
            rows_ref[to * ROWS_DEV : (to + 1) * ROWS_DEV, col * LANES : (col + 1) * LANES] = piece

    down, along = iota((LANES, 512), 0), iota((LANES, 512), 1)
    wanted = (step * INSTS + down // 16) * CAP + down % 2
    place = jnp.broadcast_to(place_ref[0:1, :], (LANES, 512))
    chosen = (place == wanted) & (along // ROWS_DEV == down // 2 % 8)
    out = dot(chosen.astype(jnp.float32).astype(jnp.bfloat16), rows_ref[...])
    out = out.astype(jnp.bfloat16)
    for i in range(INSTS):
        for col in range(TILES):
            out_ref[i * 160 + col * 16 : i * 160 + (col + 1) * 16, :] = out[
                i * 16 : (i + 1) * 16, col * LANES : (col + 1) * LANES
            ]


def dispatch(me, targets, queries, keyvals):
    rows = N_INST * N_TP * MESSAGE
    return pl.pallas_call(
        dispatch_kernel,
        out_shape=jax.ShapeDtypeStruct((rows, LANES), jnp.bfloat16),
        grid_spec=pltpu.PrefetchScalarGridSpec(
            num_scalar_prefetch=1,
            grid=(N_INST // INSTS,),
            in_specs=[
                pl.BlockSpec((8, LANES), lambda s, me: (me[0] // 16, 0)),
                pl.BlockSpec((ROWS_DEV, H * HD), lambda s, me: (0, 0)),
                pl.BlockSpec((ROWS_DEV * KVH, 2 * HD), lambda s, me: (0, 0)),
            ],
            out_specs=pl.BlockSpec((rows * INSTS // N_INST, LANES), lambda s, me: (s, 0)),
            scratch_shapes=[
                pltpu.VMEM((8, 512), jnp.int32),
                pltpu.VMEM((512, TILES * LANES), jnp.bfloat16),
            ],
        ),
        compiler_params=pltpu.CompilerParams(vmem_limit_bytes=VMEM),
        name="dispatch",
    )(me, targets, queries, keyvals)


def decode_kernel(
    info_ref, lens_ref, table_ref, queries_ref, fresh_ref, came_ref, cache_ref, target_ref,
    out_ref, bias_ref, valid_ref,
):
    inst, moved = info_ref[0], info_ref[1]
    rows = STEPS * REQ
    traded = iota((rows, 1), 0) % REQ == moved

    def merged(own, lanes):
        came = came_ref[:, lanes].astype(jnp.float32)
        came = jnp.broadcast_to(came[:, None, :], (STEPS, REQ, came.shape[1]))
        came = came.reshape(rows, came.shape[2])
        return jnp.where(traded, came, own.astype(jnp.float32)).astype(jnp.bfloat16)

    queries = merged(queries_ref[...], slice(0, GROUP * HD))
    fresh = merged(fresh_ref[...], slice(GROUP * HD, (GROUP + 2) * HD))
    query = jnp.concatenate([queries[:, g * HD : (g + 1) * HD] for g in range(GROUP)], axis=0)
    n = GROUP * rows
    row = iota((n, 1), 0)
    request, moment = row % REQ, row // REQ % STEPS
    newer = dot(query, fresh[:, :HD], NT)
    along = iota((n, rows), 1)
    newer = jnp.where((along % REQ == request) & (along // REQ <= moment), newer, MASKED)
    past = jnp.zeros((n, CTX), jnp.float32)
    length = jnp.zeros((n, 1), jnp.int32)
    values = []
    for r in range(REQ):
        pages = [
            cache_ref[pl.ds(pl.multiple_of(table_ref[r, j] * PAGE, PAGE), PAGE), :]
            for j in range(MAXP)
        ]
        context = jnp.concatenate(pages, axis=0)
        values.append(context[:, HD:])
        past = jnp.where(request == r, dot(query, context[:, :HD], NT), past)
        length = jnp.where(request == r, lens_ref[inst * REQ + r], length)
    past = jnp.where(iota((n, CTX), 1) < length, past, MASKED)
    top = jnp.maximum(
        jnp.max(past, axis=1, keepdims=True), jnp.max(newer, axis=1, keepdims=True)
    )
    past = jnp.exp2((past - top) * LOG2_SCALE)
    newer = jnp.exp2((newer - top) * LOG2_SCALE)
    total = jnp.sum(past, axis=1, keepdims=True) + jnp.sum(newer, axis=1, keepdims=True)
    past, newer = past / total, newer / total
    out = dot(newer.astype(jnp.bfloat16), fresh[:, HD:])
    for r in range(REQ):
        weights = jnp.where(request == r, past, 0.0).astype(jnp.bfloat16)
        out = out + dot(weights, values[r])
    for g in range(GROUP):
        out_ref[:, g * HD : (g + 1) * HD] = out[g * rows : (g + 1) * rows].astype(jnp.bfloat16)

    lines = target_ref.shape[0]
    hits = (target_ref[...] == inst).astype(jnp.float32).astype(jnp.bfloat16)
    slot, along = iota((SLOTS, lines), 0), iota((SLOTS, lines), 1)
    spread = dot((slot // 4 == along).astype(jnp.float32).astype(jnp.bfloat16), hits)
    slot, along = iota((SLOTS, LANES), 0), iota((SLOTS, LANES), 1)
    spread = jnp.where(along // ROWS_DEV == slot // 2 % 2, spread, 0.0).astype(jnp.bfloat16)
    count = dot(spread, jnp.ones((LANES, LANES), jnp.bfloat16))
    valid_ref[...] = (count > (slot % 2).astype(jnp.float32)).astype(jnp.float32)
    count = dot(jnp.ones((8, LANES), jnp.bfloat16), spread, NT)
    rank = (iota((8, SLOTS), 1) % 2).astype(jnp.float32)
    bias_ref[...] = jnp.where(count > rank, 0.0, MASKED)


def decode(info, lens, table, queries, fresh, came, cache, targets):
    smem, vmem = (pl.BlockSpec(memory_space=s) for s in (pltpu.SMEM, pltpu.VMEM))
    return pl.pallas_call(
        decode_kernel,
        out_shape=(
            jax.ShapeDtypeStruct(queries.shape, jnp.bfloat16),
            jax.ShapeDtypeStruct((8, SLOTS), jnp.float32),
            jax.ShapeDtypeStruct((SLOTS, LANES), jnp.float32),
        ),
        in_specs=[smem, smem, smem, vmem, vmem, vmem, vmem, vmem],
        out_specs=(vmem, vmem, vmem),
        compiler_params=pltpu.CompilerParams(vmem_limit_bytes=VMEM),
        name="decode",
    )(info, lens, table, queries, fresh, came, cache, targets)


BLOCK = 256


def prefill_kernel(arrived_ref, bias_ref, valid_ref, out_ref, packed_ref, causal_ref):
    step = pl.program_id(0)

    @pl.when(step == 0)
    def _():
        size = N_TP * MESSAGE
        to, src = iota((size, size), 0), iota((size, size), 1)
        order = (
            (to // 16 == src // 2 % TILES) & (to // 2 % 8 == src // MESSAGE) & (to % 2 == src % 2)
        )
        order = order.astype(jnp.float32).astype(jnp.bfloat16)
        for i in range(0, N_INST, 8):
            rows = jnp.concatenate(
                [arrived_ref[(i + j) * size : (i + j + 1) * size, :] for j in range(8)], axis=1
            )
            rows = dot(order, rows).astype(jnp.bfloat16)
            for tile in range(TILES):
                for j in range(8):
                    packed_ref[tile, (i + j) * 16 : (i + j + 1) * 16, :] = rows[
                        tile * 16 : (tile + 1) * 16, j * LANES : (j + 1) * LANES
                    ]
        causal_ref[...] = jnp.where(
            iota((BLOCK, BLOCK), 1) <= iota((BLOCK, BLOCK), 0), 0.0, MASKED
        )

    def block(start):
        end = start + BLOCK
        keys, values = packed_ref[GROUP, :end, :], packed_ref[GROUP + 1, :end, :]
        bias = bias_ref[0:1, :end]
        own = causal_ref[...] + bias[:, start:]
        filled = valid_ref[start:end, 0:1]
        for h in range(GROUP):
            scores = dot(packed_ref[h, start:end, :], keys, NT)
            last = scores[:, start:] + own
            top = jnp.max(last, axis=1, keepdims=True)
            if start:
                scores = scores[:, :start] + bias[:, :start]
                top = jnp.maximum(top, jnp.max(scores, axis=1, keepdims=True))
                scores = jnp.concatenate([scores, last], axis=1)
            else:
                scores = last
            expo = jnp.exp2((scores - top) * LOG2_SCALE)
            share = filled / jnp.sum(expo, axis=1, keepdims=True)
            out = dot((expo * share).astype(jnp.bfloat16), values)
            out_ref[:, h * HD : (h + 1) * HD] = out.astype(jnp.bfloat16)

    for i in range(SLOTS // BLOCK):
        pl.when(step == i)(functools.partial(block, i * BLOCK))


def prefill(arrived, bias, valid):
    whole = lambda s: (0, 0)
    return pl.pallas_call(
        prefill_kernel,
        out_shape=jax.ShapeDtypeStruct((SLOTS, GROUP * HD), jnp.bfloat16),
        grid=(SLOTS // BLOCK,),
        in_specs=[pl.BlockSpec(x.shape, whole) for x in (arrived, bias, valid)],
        out_specs=pl.BlockSpec((BLOCK, GROUP * HD), lambda s: (s, 0)),
        scratch_shapes=[
            pltpu.VMEM((TILES, SLOTS, LANES), jnp.bfloat16),
            pltpu.VMEM((BLOCK, BLOCK), jnp.float32),
        ],
        compiler_params=pltpu.CompilerParams(vmem_limit_bytes=VMEM),
        name="prefill",
    )(arrived, bias, valid)


def exchanged(array, distance):
    found = jnp.zeros_like(array)
    for bit in range(N_INST.bit_length() - 1):
        pairs = [(i, i ^ 1 << bit) for i in range(N_INST)]
        found = jnp.where(distance == 1 << bit, lax.ppermute(array, "inst", pairs), found)
    return found


def local(
    step_queries,
    step_keyvals,
    cache_pages,
    block_table,
    context_len,
    partner,
    moved_slot,
    prompt_queries,
    prompt_keyvals,
    prompt_target,
):
    inst = lax.axis_index("inst")
    device = inst * N_TP + lax.axis_index("tp")
    targets = prompt_target.reshape(-1, LANES)
    sent = dispatch(
        device[None], targets, prompt_queries, prompt_keyvals.reshape(ROWS_DEV * KVH, 2 * HD)
    )
    arrived = lax.all_to_all(
        sent.reshape(N_INST * N_TP, MESSAGE // 4, 4, LANES), ("inst", "tp"), 0, 0, tiled=True
    ).reshape(sent.shape)

    moved = moved_slot[inst]
    distance = inst ^ partner[inst]
    queries = step_queries.reshape(STEPS * REQ, GROUP * HD)
    fresh = step_keyvals.reshape(STEPS * REQ, 2 * HD)
    traded = jnp.concatenate(
        [
            lax.dynamic_index_in_dim(step_queries, moved, 1, keepdims=False),
            lax.dynamic_index_in_dim(step_keyvals[:, :, 0], moved, 1, keepdims=False),
        ],
        axis=1,
    )
    came = exchanged(traded, distance)
    info = jnp.stack([inst, moved])
    decoded, bias, valid = decode(
        info, context_len, block_table, queries, fresh, came,
        cache_pages.reshape(POOL * PAGE, 2 * HD), targets,
    )
    decoded = decoded.reshape(STEPS, REQ, GROUP * HD)
    back = exchanged(lax.dynamic_index_in_dim(decoded, moved, 1, keepdims=False), distance)
    here = (jnp.arange(REQ, dtype=jnp.int32) == moved)[None, :, None]
    decode_output = jnp.where(here, back[:, None, :], decoded)
    return decode_output, prefill(arrived, bias, valid)


def solution(mesh):
    placed = (
        P(None, "inst", "tp"),
        P(None, "inst", "tp", None),
        P("inst", None, "tp", None),
        P("inst", None),
        P(),
        P(),
        P(),
        P(("inst", "tp"), None),
        P(("inst", "tp"), None, None),
        P(),
    )
    return jax.shard_map(
        local,
        mesh=mesh,
        in_specs=placed,
        out_specs=(P(None, "inst", "tp"), P("inst", "tp")),
        check_vma=False,
    )
```

time: 246 us -> 152 us (0.62)
  the two profiles are of different devices: /device:TPU:1 before, /device:TPU:16 now
where the time goes in v1:
time: 152 us; the launch traced here: 151 us
  starting transfers between devices  80.2 us (53%)
  waiting for transfers between devices  32.2 us (21%)
  Pallas kernels  25.8 us (17%)
  local copies, waits for them, and re-layouts  7.14 us (5%)
  between operations  3.66 us (2%)
  other arithmetic  2.13 us (1%)
    ppermute x12, starting transfers between devices, exchanged(): lax.ppermute(array, 'inst', pairs)  59.2 us
    ppermute x12, waiting for transfers between devices, exchanged(): lax.ppermute(array, 'inst', pairs)  32.1 us
    all_to_all x1, starting transfers between devices, local(): lax.all_to_all(sent.reshape(N_INST * N_TP, MESSAGE // 4, 4, LANES), ('ins...  21 us
    pallas_call x1, Pallas kernels, prefill(): pl.pallas_call(prefill_kernel, out_shape=jax.ShapeDtypeStruct((SLOTS, GRO...  20.4 us
    unnamed x27, local copies, waits for them, and re-layouts  5.83 us
    pallas_call x1, Pallas kernels, dispatch(): pl.pallas_call(dispatch_kernel, out_shape=jax.ShapeDtypeStruct((rows, LAN...  3.3 us
  transfers between devices with their start and end apart: 13, of which 2 were waited for; matrix products, arithmetic and copies ran while one was open for 2% of the time, Pallas kernels for 1%

profile of v1, /device:TPU:16, one launch (start us, length us, event | category | flops | bytes accessed | tf_op | source)
XLA Modules:
  0.0 151.0 jit_solution(14423053111968585816)
XLA Ops:
  0.6 0.0 copy-start.2
  0.6 1.2 copy-done.2
  1.9 0.9 copy-done.3
  2.8 0.9 copy-done.5
  3.7 3.3 %dispatch.1 = bf16[10240,128]{1,0:T(8,128)(2,1)S(1)} custom-call(s32[1]{0:T(128)} %bitcast.8.me_ref, s32[256,128]{1,0:T(8,128)S(1)} %bitcast.25, bf16[64,8192]{1,0:T(8,128)(2,1)S(1)} %copy-done.2, bf16[512,256]{1,0:T(8,128)(2,1)S(1)} %bitcast.27), custom_call_target="tpu_custom_call" | custom-call | tf_op jit(solution)/shard_map/dispatch/pallas_call | solution.py:90
  7.0 0.0 copy-start
  7.0 1.5 copy-done
  8.5 0.0 copy-start.4
  8.5 0.0 copy-start.8
  8.6 0.0 copy-start.9
  8.6 21.0 %all-to-all-start = ((bf16[512,5,4,128]{3,2,1,0:T(4,128)(2,1)}), bf16[512,5,4,128]{3,2,1,0:T(4,128)(2,1)S(1)}, u32[]{:S(2)}, u32[]{:S(2)}) async-start(bf16[512,5,4,128]{3,2,1,0:T(4,128)(2,1)} %bitcast.23), calls=%async_computation | async-start | bytes 5242880 | tf_op jit(solution)/shard_map/all_to_all | solution.py:287
  29.6 0.6 dynamic_slice.17
  32.2 3.4 %collective-permute-start.5 = (bf16[4,1280]{1,0:T(4,128)(2,1)S(1)}, bf16[4,1280]{1,0:T(4,128)(2,1)S(1)}, u32[]{:S(2)}, u32[]{:S(2)}) collective-permute-start(bf16[4,1280]{1,0:T(4,128)(2,1)S(1)} %pad_maximum_fusion), channel_id=1, source_target_pairs={{0,8},{8,0},{16,24},{24,16},{32,40},{40,32},{48,56},{56,48},{64,72... | collective-permute-start | bytes 30728 | tf_op jit(solution)/shard_map/ppermute | solution.py:265
  35.7 4.7 %collective-permute-start.4 = (bf16[4,1280]{1,0:T(4,128)(2,1)S(1)}, bf16[4,1280]{1,0:T(4,128)(2,1)S(1)}, u32[]{:S(2)}, u32[]{:S(2)}) collective-permute-start(bf16[4,1280]{1,0:T(4,128)(2,1)S(1)} %pad_maximum_fusion), channel_id=1, source_target_pairs={{0,16},{8,24},{16,0},{24,8},{32,48},{40,56},{48,32},{56,40},{64,80... | collective-permute-start | bytes 30728 | tf_op jit(solution)/shard_map/ppermute | solution.py:265
  40.4 4.3 %collective-permute-start.3 = (bf16[4,1280]{1,0:T(4,128)(2,1)S(1)}, bf16[4,1280]{1,0:T(4,128)(2,1)S(1)}, u32[]{:S(2)}, u32[]{:S(2)}) collective-permute-start(bf16[4,1280]{1,0:T(4,128)(2,1)S(1)} %pad_maximum_fusion), channel_id=1, source_target_pairs={{0,32},{8,40},{16,48},{24,56},{32,0},{40,8},{48,16},{56,24},{64,96... | collective-permute-start | bytes 30728 | tf_op jit(solution)/shard_map/ppermute | solution.py:265
  44.7 3.4 %collective-permute-start.2 = (bf16[4,1280]{1,0:T(4,128)(2,1)S(1)}, bf16[4,1280]{1,0:T(4,128)(2,1)S(1)}, u32[]{:S(2)}, u32[]{:S(2)}) collective-permute-start(bf16[4,1280]{1,0:T(4,128)(2,1)S(1)} %pad_maximum_fusion), channel_id=1, source_target_pairs={{0,64},{8,72},{16,80},{24,88},{32,96},{40,104},{48,112},{56,120},{... | collective-permute-start | bytes 30728 | tf_op jit(solution)/shard_map/ppermute | solution.py:265
  48.1 4.6 %collective-permute-start.1 = (bf16[4,1280]{1,0:T(4,128)(2,1)S(1)}, bf16[4,1280]{1,0:T(4,128)(2,1)S(1)}, u32[]{:S(2)}, u32[]{:S(2)}) collective-permute-start(bf16[4,1280]{1,0:T(4,128)(2,1)S(1)} %pad_maximum_fusion), channel_id=1, source_target_pairs={{0,128},{8,136},{16,144},{24,152},{32,160},{40,168},{48,176},{56,1... | collective-permute-start | bytes 30728 | tf_op jit(solution)/shard_map/ppermute | solution.py:265
  52.7 30.7 %collective-permute-done.5 = bf16[4,1280]{1,0:T(4,128)(2,1)S(1)} collective-permute-done((bf16[4,1280]{1,0:T(4,128)(2,1)S(1)}, bf16[4,1280]{1,0:T(4,128)(2,1)S(1)}, u32[]{:S(2)}, u32[]{:S(2)}) %collective-permute-start.5) | collective-permute-done | bytes 10272 | tf_op jit(solution)/shard_map/ppermute | solution.py:265
  83.4 9.4 %collective-permute-start = (bf16[4,1280]{1,0:T(4,128)(2,1)S(1)}, bf16[4,1280]{1,0:T(4,128)(2,1)S(1)}, u32[]{:S(2)}, u32[]{:S(2)}) collective-permute-start(bf16[4,1280]{1,0:T(4,128)(2,1)S(1)} %pad_maximum_fusion), channel_id=1, source_target_pairs={{0,256},{8,264},{16,272},{24,280},{32,288},{40,296},{48,304},{56,3... | collective-permute-start | bytes 30728 | tf_op jit(solution)/shard_map/ppermute | solution.py:265
  92.8 0.7 pad_add_fusion.info_ref
  93.5 0.7 dynamic_slice.18
  94.9 0.0 collective-permute-done.4
  94.9 0.0 collective-permute-done.3
  94.9 0.0 collective-permute-done.2
  94.9 0.0 collective-permute-done.1
  94.9 0.0 collective-permute-done
  95.0 0.0 copy-done.4
  95.0 0.0 copy-done.8
  95.0 0.0 copy-done.9
  95.0 0.0 copy-start.1
  95.0 1.2 copy-done.1
  96.2 2.1 %decode.1 = (bf16[32,1024]{1,0:T(8,128)(2,1)S(1)}, f32[8,1024]{1,0:T(8,128)S(1)}, f32[1024,128]{1,0:T(8,128)S(1)}) custom-call(s32[2]{0:T(128)S(1)} %pad_add_fusion.info_ref, s32[512]{0:T(512)S(1)} %copy-done.9, s32[8,16]{1,0:T(8,128)S(1)} %copy-done.8, bf16[32,1024]{1,0:T(8,128)(2,1)S(1)} %bitcast.28, bf16[32,256]{1,0:T(8,128)(2,1)S(1)} %bitcast.30, ...), custom_call_target="tpu_custom_call" | custom-call | tf_op jit(solution)/shard_map/decode/pallas_call | solution.py:177
  98.4 4.3 %collective-permute-start.11 = (bf16[4,1024]{1,0:T(4,128)(2,1)S(1)}, bf16[4,1024]{1,0:T(4,128)(2,1)S(1)}, u32[]{:S(2)}, u32[]{:S(2)}) collective-permute-start(bf16[4,1024]{1,0:T(4,128)(2,1)S(1)} %bitcast.32), channel_id=1, source_target_pairs={{0,8},{8,0},{16,24},{24,16},{32,40},{40,32},{48,56},{56,48},{64,72... | collective-permute-start | bytes 24584 | tf_op jit(solution)/shard_map/ppermute | solution.py:265
  102.7 1.9 %collective-permute-start.10 = (bf16[4,1024]{1,0:T(4,128)(2,1)S(1)}, bf16[4,1024]{1,0:T(4,128)(2,1)S(1)}, u32[]{:S(2)}, u32[]{:S(2)}) collective-permute-start(bf16[4,1024]{1,0:T(4,128)(2,1)S(1)} %bitcast.33), channel_id=1, source_target_pairs={{0,16},{8,24},{16,0},{24,8},{32,48},{40,56},{48,32},{56,40},{64,80... | collective-permute-start | bytes 24584 | tf_op jit(solution)/shard_map/ppermute | solution.py:265
  104.6 7.8 %collective-permute-start.9 = (bf16[4,1024]{1,0:T(4,128)(2,1)S(1)}, bf16[4,1024]{1,0:T(4,128)(2,1)S(1)}, u32[]{:S(2)}, u32[]{:S(2)}) collective-permute-start(bf16[4,1024]{1,0:T(4,128)(2,1)S(1)} %bitcast.34), channel_id=1, source_target_pairs={{0,32},{8,40},{16,48},{24,56},{32,0},{40,8},{48,16},{56,24},{64,96... | collective-permute-start | bytes 24584 | tf_op jit(solution)/shard_map/ppermute | solution.py:265
  112.4 3.4 %collective-permute-start.8 = (bf16[4,1024]{1,0:T(4,128)(2,1)S(1)}, bf16[4,1024]{1,0:T(4,128)(2,1)S(1)}, u32[]{:S(2)}, u32[]{:S(2)}) collective-permute-start(bf16[4,1024]{1,0:T(4,128)(2,1)S(1)} %bitcast.35), channel_id=1, source_target_pairs={{0,64},{8,72},{16,80},{24,88},{32,96},{40,104},{48,112},{56,120},{... | collective-permute-start | bytes 24584 | tf_op jit(solution)/shard_map/ppermute | solution.py:265
  115.8 4.6 %collective-permute-start.7 = (bf16[4,1024]{1,0:T(4,128)(2,1)S(1)}, bf16[4,1024]{1,0:T(4,128)(2,1)S(1)}, u32[]{:S(2)}, u32[]{:S(2)}) collective-permute-start(bf16[4,1024]{1,0:T(4,128)(2,1)S(1)} %bitcast.36), channel_id=1, source_target_pairs={{0,128},{8,136},{16,144},{24,152},{32,160},{40,168},{48,176},{56,1... | collective-permute-start | bytes 24584 | tf_op jit(solution)/shard_map/ppermute | solution.py:265
  120.4 0.0 collective-permute-done.11
  120.4 7.3 %collective-permute-start.6 = (bf16[4,1024]{1,0:T(4,128)(2,1)S(1)}, bf16[4,1024]{1,0:T(4,128)(2,1)S(1)}, u32[]{:S(2)}, u32[]{:S(2)}) collective-permute-start(bf16[4,1024]{1,0:T(4,128)(2,1)S(1)} %bitcast.37), channel_id=1, source_target_pairs={{0,256},{8,264},{16,272},{24,280},{32,288},{40,296},{48,304},{56,3... | collective-permute-start | bytes 24584 | tf_op jit(solution)/shard_map/ppermute | solution.py:265
  127.8 0.7 iota_compare_fusion
  128.4 0.0 collective-permute-done.10
  128.4 0.0 collective-permute-done.9
  128.4 0.0 collective-permute-done.8
  128.5 0.0 collective-permute-done.7
  128.5 1.4 collective-permute-done.6
  129.9 0.7 broadcast_select_fusion
  130.6 0.0 all-to-all-done
  130.6 20.4 %prefill.1 = bf16[1024,1024]{1,0:T(8,128)(2,1)} custom-call(bf16[10240,128]{1,0:T(8,128)(2,1)S(1)} %bitcast.22, f32[8,1024]{1,0:T(8,128)S(1)} %get-tuple-element.6.bias_ref, f32[1024,128]{1,0:T(8,128)S(1)} %get-tuple-element.7.valid_ref), custom_call_target="tpu_custom_call" | custom-call | tf_op jit(solution)/shard_map/prefill/pallas_call | solution.py:246
  (19 shorter events, 0.1 us)
Async XLA Ops:
  0.6 1.2 copy-start.2
  1.9 0.9 copy-start.3
  2.8 0.9 copy-start.5
  7.0 1.5 copy-start
  8.5 21.1 %copy-start.10 = (s32[64]{0:T(128)S(1)}, s32[64]{0:T(128)}, u32[]{:S(2)}) copy-start(s32[64]{0:T(128)} %param.16) | copy-start | bytes 772
  8.5 23.6 %copy-start.7 = (bf16[4,8,1,256]{3,1,2,0:T(8,128)(2,1)S(1)}, bf16[4,8,1,256]{3,1,2,0:T(8,128)(2,1)}, u32[]{:S(2)}) copy-start(bf16[4,8,1,256]{3,1,2,0:T(8,128)(2,1)} %param.11) | copy-start | bytes 49156
  8.5 23.6 %copy-start.6 = (bf16[4,8,1024]{2,1,0:T(8,128)(2,1)S(1)}, bf16[4,8,1024]{2,1,0:T(8,128)(2,1)}, u32[]{:S(2)}) copy-start(bf16[4,8,1024]{2,1,0:T(8,128)(2,1)} %param.10) | copy-start | bytes 196612
  8.5 85.0 %copy-start.11 = (s32[64]{0:T(128)S(1)}, s32[64]{0:T(128)}, u32[]{:S(2)}) copy-start(s32[64]{0:T(128)} %param.15) | copy-start | bytes 772
  8.5 86.4 %copy-start.4 = (s32[32768,1]{0,1:T(1,128)S(1)}, s32[32768,1]{0,1:T(1,128)}, u32[]{:S(2)}) copy-start(s32[32768,1]{0,1:T(1,128)} %param.19) | copy-start | bytes 393220
  8.5 86.4 %copy-start.8 = (s32[8,16]{1,0:T(8,128)S(1)}, s32[8,16]{1,0:T(8,128)}, u32[]{:S(2)}) copy-start(s32[8,16]{1,0:T(8,128)} %table_ref.1) | copy-start | bytes 1540
  8.6 86.4 %copy-start.9 = (s32[512]{0:T(512)S(1)}, s32[512]{0:T(512)}, u32[]{:S(2)}) copy-start(s32[512]{0:T(512)} %lens_ref.1) | copy-start | bytes 6148
  8.6 122.1 %all-to-all-start = ((bf16[512,5,4,128]{3,2,1,0:T(4,128)(2,1)}), bf16[512,5,4,128]{3,2,1,0:T(4,128)(2,1)S(1)}, u32[]{:S(2)}, u32[]{:S(2)}) async-start(bf16[512,5,4,128]{3,2,1,0:T(4,128)(2,1)} %bitcast.23), calls=%async_computation | async-start | bytes 5242880 | tf_op jit(solution)/shard_map/all_to_all | solution.py:287
  32.2 51.1 %collective-permute-start.5 = (bf16[4,1280]{1,0:T(4,128)(2,1)S(1)}, bf16[4,1280]{1,0:T(4,128)(2,1)S(1)}, u32[]{:S(2)}, u32[]{:S(2)}) collective-permute-start(bf16[4,1280]{1,0:T(4,128)(2,1)S(1)} %pad_maximum_fusion), channel_id=1, source_target_pairs={{0,8},{8,0},{16,24},{24,16},{32,40},{40,32},{48,56},{56,48},{64,72... | collective-permute-start | bytes 30728 | tf_op jit(solution)/shard_map/ppermute | solution.py:265
  35.7 59.2 %collective-permute-start.4 = (bf16[4,1280]{1,0:T(4,128)(2,1)S(1)}, bf16[4,1280]{1,0:T(4,128)(2,1)S(1)}, u32[]{:S(2)}, u32[]{:S(2)}) collective-permute-start(bf16[4,1280]{1,0:T(4,128)(2,1)S(1)} %pad_maximum_fusion), channel_id=1, source_target_pairs={{0,16},{8,24},{16,0},{24,8},{32,48},{40,56},{48,32},{56,40},{64,80... | collective-permute-start | bytes 30728 | tf_op jit(solution)/shard_map/ppermute | solution.py:265
  40.4 54.5 %collective-permute-start.3 = (bf16[4,1280]{1,0:T(4,128)(2,1)S(1)}, bf16[4,1280]{1,0:T(4,128)(2,1)S(1)}, u32[]{:S(2)}, u32[]{:S(2)}) collective-permute-start(bf16[4,1280]{1,0:T(4,128)(2,1)S(1)} %pad_maximum_fusion), channel_id=1, source_target_pairs={{0,32},{8,40},{16,48},{24,56},{32,0},{40,8},{48,16},{56,24},{64,96... | collective-permute-start | bytes 30728 | tf_op jit(solution)/shard_map/ppermute | solution.py:265
  44.7 50.2 %collective-permute-start.2 = (bf16[4,1280]{1,0:T(4,128)(2,1)S(1)}, bf16[4,1280]{1,0:T(4,128)(2,1)S(1)}, u32[]{:S(2)}, u32[]{:S(2)}) collective-permute-start(bf16[4,1280]{1,0:T(4,128)(2,1)S(1)} %pad_maximum_fusion), channel_id=1, source_target_pairs={{0,64},{8,72},{16,80},{24,88},{32,96},{40,104},{48,112},{56,120},{... | collective-permute-start | bytes 30728 | tf_op jit(solution)/shard_map/ppermute | solution.py:265
  48.1 46.9 %collective-permute-start.1 = (bf16[4,1280]{1,0:T(4,128)(2,1)S(1)}, bf16[4,1280]{1,0:T(4,128)(2,1)S(1)}, u32[]{:S(2)}, u32[]{:S(2)}) collective-permute-start(bf16[4,1280]{1,0:T(4,128)(2,1)S(1)} %pad_maximum_fusion), channel_id=1, source_target_pairs={{0,128},{8,136},{16,144},{24,152},{32,160},{40,168},{48,176},{56,1... | collective-permute-start | bytes 30728 | tf_op jit(solution)/shard_map/ppermute | solution.py:265
  83.4 11.6 %collective-permute-start = (bf16[4,1280]{1,0:T(4,128)(2,1)S(1)}, bf16[4,1280]{1,0:T(4,128)(2,1)S(1)}, u32[]{:S(2)}, u32[]{:S(2)}) collective-permute-start(bf16[4,1280]{1,0:T(4,128)(2,1)S(1)} %pad_maximum_fusion), channel_id=1, source_target_pairs={{0,256},{8,264},{16,272},{24,280},{32,288},{40,296},{48,304},{56,3... | collective-permute-start | bytes 30728 | tf_op jit(solution)/shard_map/ppermute | solution.py:265
  95.0 1.2 copy-start.1
  98.4 22.1 %collective-permute-start.11 = (bf16[4,1024]{1,0:T(4,128)(2,1)S(1)}, bf16[4,1024]{1,0:T(4,128)(2,1)S(1)}, u32[]{:S(2)}, u32[]{:S(2)}) collective-permute-start(bf16[4,1024]{1,0:T(4,128)(2,1)S(1)} %bitcast.32), channel_id=1, source_target_pairs={{0,8},{8,0},{16,24},{24,16},{32,40},{40,32},{48,56},{56,48},{64,72... | collective-permute-start | bytes 24584 | tf_op jit(solution)/shard_map/ppermute | solution.py:265
  102.7 25.8 %collective-permute-start.10 = (bf16[4,1024]{1,0:T(4,128)(2,1)S(1)}, bf16[4,1024]{1,0:T(4,128)(2,1)S(1)}, u32[]{:S(2)}, u32[]{:S(2)}) collective-permute-start(bf16[4,1024]{1,0:T(4,128)(2,1)S(1)} %bitcast.33), channel_id=1, source_target_pairs={{0,16},{8,24},{16,0},{24,8},{32,48},{40,56},{48,32},{56,40},{64,80... | collective-permute-start | bytes 24584 | tf_op jit(solution)/shard_map/ppermute | solution.py:265
  104.6 23.8 %collective-permute-start.9 = (bf16[4,1024]{1,0:T(4,128)(2,1)S(1)}, bf16[4,1024]{1,0:T(4,128)(2,1)S(1)}, u32[]{:S(2)}, u32[]{:S(2)}) collective-permute-start(bf16[4,1024]{1,0:T(4,128)(2,1)S(1)} %bitcast.34), channel_id=1, source_target_pairs={{0,32},{8,40},{16,48},{24,56},{32,0},{40,8},{48,16},{56,24},{64,96... | collective-permute-start | bytes 24584 | tf_op jit(solution)/shard_map/ppermute | solution.py:265
  112.4 16.0 %collective-permute-start.8 = (bf16[4,1024]{1,0:T(4,128)(2,1)S(1)}, bf16[4,1024]{1,0:T(4,128)(2,1)S(1)}, u32[]{:S(2)}, u32[]{:S(2)}) collective-permute-start(bf16[4,1024]{1,0:T(4,128)(2,1)S(1)} %bitcast.35), channel_id=1, source_target_pairs={{0,64},{8,72},{16,80},{24,88},{32,96},{40,104},{48,112},{56,120},{... | collective-permute-start | bytes 24584 | tf_op jit(solution)/shard_map/ppermute | solution.py:265
  115.8 12.6 %collective-permute-start.7 = (bf16[4,1024]{1,0:T(4,128)(2,1)S(1)}, bf16[4,1024]{1,0:T(4,128)(2,1)S(1)}, u32[]{:S(2)}, u32[]{:S(2)}) collective-permute-start(bf16[4,1024]{1,0:T(4,128)(2,1)S(1)} %bitcast.36), channel_id=1, source_target_pairs={{0,128},{8,136},{16,144},{24,152},{32,160},{40,168},{48,176},{56,1... | collective-permute-start | bytes 24584 | tf_op jit(solution)/shard_map/ppermute | solution.py:265
  120.4 9.5 %collective-permute-start.6 = (bf16[4,1024]{1,0:T(4,128)(2,1)S(1)}, bf16[4,1024]{1,0:T(4,128)(2,1)S(1)}, u32[]{:S(2)}, u32[]{:S(2)}) collective-permute-start(bf16[4,1024]{1,0:T(4,128)(2,1)S(1)} %bitcast.37), channel_id=1, source_target_pairs={{0,256},{8,264},{16,272},{24,280},{32,288},{40,296},{48,304},{56,3... | collective-permute-start | bytes 24584 | tf_op jit(solution)/shard_map/ppermute | solution.py:265

commit v2 on v1

v2 whole, which is shorter than its diff:
```python
import functools
import math

import jax
import jax.numpy as jnp
from jax import lax
from jax.experimental import pallas as pl
from jax.experimental.pallas import tpu as pltpu
from jax.sharding import PartitionSpec as P

H, KVH, HD = 64, 8, 128
REQ, PAGE, MAXP, STEPS = 8, 16, 16, 4
ROWS_DEV, CTX, POOL, CAP, SLOTS = 64, 256, 128, 2, 1024
N_INST, N_TP = 64, 8
GROUP = H // KVH
TILES = GROUP + 2
MESSAGE = TILES * CAP
LANES = 128
LOG2_SCALE = HD**-0.5 * math.log2(math.e)
MASKED = -1e30
VMEM = 48 * 1024 * 1024


def iota(shape, dim):
    return lax.broadcasted_iota(jnp.int32, shape, dim)


def dot(a, b, contract=((1,), (0,))):
    return lax.dot_general(a, b, (contract, ((), ())), preferred_element_type=jnp.float32)


NT = ((1,), (1,))


INSTS = 8


def dispatch_kernel(me_ref, target_ref, queries_ref, keyvals_ref, out_ref, place_ref, rows_ref):
    step = pl.program_id(0)

    @pl.when(step == 0)
    def _():
        me = me_ref[0]
        line = lax.rem(lax.div(me, 2), 8)
        both = jnp.sum(
            jnp.where(iota((8, LANES), 0) == line, target_ref[...], 0), axis=0, keepdims=True
        )
        both = jnp.broadcast_to(both, (8, LANES))
        other = pltpu.roll(both, ROWS_DEV, 1)
        first = iota((8, LANES), 1) < ROWS_DEV
        odd = lax.rem(me, 2) == 1
        mine = jnp.where(first != odd, both, other)[0:1]
        down, along = iota((ROWS_DEV, LANES), 0), iota((ROWS_DEV, LANES), 1)
        wide = jnp.broadcast_to(mine, (ROWS_DEV, LANES))
        column = jnp.sum(jnp.where(down == along, wide, 0), axis=1, keepdims=True)
        earlier = (column == wide) & (down < along % ROWS_DEV)
        rank = jnp.sum(earlier.astype(jnp.int32), axis=0, keepdims=True)
        place = jnp.broadcast_to(mine * CAP + rank, (8, LANES))
        for i in range(4):
            place_ref[:, i * LANES : (i + 1) * LANES] = place
        down, along = iota((512, 512), 0), iota((512, 512), 1)
        order = (down % ROWS_DEV == along // KVH) & (down // ROWS_DEV == along % KVH)
        keyvals = dot(order.astype(jnp.float32).astype(jnp.bfloat16), keyvals_ref[...])
        keyvals = keyvals.astype(jnp.bfloat16)
        for c in range(N_TP * TILES):
            tp, tile = divmod(c, TILES)
            if tile < GROUP:
                piece = queries_ref[:, (tp * GROUP + tile) * HD : (tp * GROUP + tile + 1) * HD]
            else:
                lane = (tile - GROUP) * HD
                piece = keyvals[tp * ROWS_DEV : (tp + 1) * ROWS_DEV, lane : lane + HD]
            to, col = c % 8, c // 8
            rows_ref[to * ROWS_DEV : (to + 1) * ROWS_DEV, col * LANES : (col + 1) * LANES] = piece

    down, along = iota((LANES, 512), 0), iota((LANES, 512), 1)
    wanted = (step * INSTS + down // 16) * CAP + down % 2
    place = jnp.broadcast_to(place_ref[0:1, :], (LANES, 512))
    chosen = (place == wanted) & (along // ROWS_DEV == down // 2 % 8)
    out = dot(chosen.astype(jnp.float32).astype(jnp.bfloat16), rows_ref[...])
    out = out.astype(jnp.bfloat16)
    for i in range(INSTS):
        for col in range(TILES):
            out_ref[i * 160 + col * 16 : i * 160 + (col + 1) * 16, :] = out[
                i * 16 : (i + 1) * 16, col * LANES : (col + 1) * LANES
            ]


def dispatch(me, targets, queries, keyvals):
    rows = N_INST * N_TP * MESSAGE
    return pl.pallas_call(
        dispatch_kernel,
        out_shape=pltpu.HBM((rows, LANES), jnp.bfloat16),
        grid_spec=pltpu.PrefetchScalarGridSpec(
            num_scalar_prefetch=1,
            grid=(N_INST // INSTS,),
            in_specs=[
                pl.BlockSpec((8, LANES), lambda s, me: (me[0] // 16, 0)),
                pl.BlockSpec((ROWS_DEV, H * HD), lambda s, me: (0, 0)),
                pl.BlockSpec((ROWS_DEV * KVH, 2 * HD), lambda s, me: (0, 0)),
            ],
            out_specs=pl.BlockSpec((rows * INSTS // N_INST, LANES), lambda s, me: (s, 0)),
            scratch_shapes=[
                pltpu.VMEM((8, 512), jnp.int32),
                pltpu.VMEM((512, TILES * LANES), jnp.bfloat16),
            ],
        ),
        compiler_params=pltpu.CompilerParams(vmem_limit_bytes=VMEM),
        name="dispatch",
    )(me, *(pltpu.with_memory_space_constraint(x, pltpu.HBM) for x in (targets, queries, keyvals)))


def prepare_kernel(
    inst_ref, slot_ref, table_ref, cache_ref, target_ref, leaving_ref, context_ref, mask_ref
):
    inst = inst_ref[0]
    moved = slot_ref[inst]
    for r in range(REQ):
        for j in range(MAXP):
            page = pl.multiple_of(table_ref[r, j] * PAGE, PAGE)
            row = r * CTX + j * PAGE
            context_ref[row : row + PAGE, :] = cache_ref[pl.ds(page, PAGE), :]
    leaving_ref[...] = context_ref[pl.ds(pl.multiple_of(moved * CTX, CTX), CTX), :]
    lines = target_ref.shape[0]
    hits = (target_ref[...] == inst).astype(jnp.float32).astype(jnp.bfloat16)
    slot, along = iota((SLOTS, lines), 0), iota((SLOTS, lines), 1)
    spread = dot((slot // 4 == along).astype(jnp.float32).astype(jnp.bfloat16), hits)
    slot, along = iota((SLOTS, LANES), 0), iota((SLOTS, LANES), 1)
    spread = jnp.where(along // ROWS_DEV == slot // 2 % 2, spread, 0.0).astype(jnp.bfloat16)
    count = dot(spread, jnp.ones((LANES, LANES), jnp.bfloat16))
    mask = jnp.where(count > (slot % 2).astype(jnp.float32), 0.0, MASKED)
    mask_ref[...] = mask.astype(jnp.bfloat16)


def specs(*spaces):
    return [pl.BlockSpec(memory_space=s) for s in spaces]


def prepare(inst, slots, table, cache, targets):
    smem, vmem = pltpu.SMEM, pltpu.VMEM
    return pl.pallas_call(
        prepare_kernel,
        out_shape=(
            jax.ShapeDtypeStruct((CTX, 2 * HD), jnp.bfloat16),
            jax.ShapeDtypeStruct((REQ * CTX, 2 * HD), jnp.bfloat16),
            jax.ShapeDtypeStruct((SLOTS, LANES), jnp.bfloat16),
        ),
        in_specs=specs(smem, smem, smem, vmem, vmem),
        out_specs=specs(vmem, vmem, vmem),
        compiler_params=pltpu.CompilerParams(vmem_limit_bytes=VMEM),
        name="prepare",
    )(inst, slots, table, cache, targets)


BITS = N_INST.bit_length() - 1


def decode_kernel(
    inst_ref, partner_ref, slot_ref, lens_ref, queries_ref, fresh_ref, context_ref, *refs
):
    *came_refs, out_ref, came_ref = refs
    inst = inst_ref[0]
    other = partner_ref[inst]
    moved = slot_ref[inst]
    for bit in range(BITS):

        @pl.when(jnp.bitwise_xor(inst, other) == 1 << bit)
        def _(bit=bit):
            came_ref[...] = came_refs[bit][...]

    rows = STEPS * REQ
    queries, fresh, came = queries_ref[...], fresh_ref[...], came_ref[...]
    query = jnp.concatenate([queries[:, g * HD : (g + 1) * HD] for g in range(GROUP)], axis=0)
    n = GROUP * rows
    row = iota((n, 1), 0)
    request, moment = row % REQ, row // REQ % STEPS
    newer = dot(query, fresh[:, :HD], NT)
    along = iota((n, rows), 1)
    newer = jnp.where((along % REQ == request) & (along // REQ <= moment), newer, MASKED)
    past = jnp.zeros((n, CTX), jnp.float32)
    length = jnp.zeros((n, 1), jnp.int32)
    values = []
    for r in range(REQ):
        context = jnp.where(moved == r, came, context_ref[r * CTX : (r + 1) * CTX, :])
        values.append(context[:, HD:])
        past = jnp.where(request == r, dot(query, context[:, :HD], NT), past)
        source = jnp.where(moved == r, other * REQ + slot_ref[other], inst * REQ + r)
        length = jnp.where(request == r, lens_ref[source], length)
    past = jnp.where(iota((n, CTX), 1) < length, past, MASKED)
    top = jnp.maximum(
        jnp.max(past, axis=1, keepdims=True), jnp.max(newer, axis=1, keepdims=True)
    )
    past = jnp.exp2((past - top) * LOG2_SCALE)
    newer = jnp.exp2((newer - top) * LOG2_SCALE)
    total = jnp.sum(past, axis=1, keepdims=True) + jnp.sum(newer, axis=1, keepdims=True)
    past, newer = past / total, newer / total
    out = dot(newer.astype(jnp.bfloat16), fresh[:, HD:])
    for r in range(REQ):
        weights = jnp.where(request == r, past, 0.0).astype(jnp.bfloat16)
        out = out + dot(weights, values[r])
    for g in range(GROUP):
        out_ref[:, g * HD : (g + 1) * HD] = out[g * rows : (g + 1) * rows].astype(jnp.bfloat16)


def decode(inst, partner, slots, lens, queries, fresh, context, came):
    smem, vmem = pltpu.SMEM, pltpu.VMEM
    return pl.pallas_call(
        decode_kernel,
        out_shape=jax.ShapeDtypeStruct(queries.shape, jnp.bfloat16),
        in_specs=specs(*[smem] * 4, *[vmem] * (3 + BITS)),
        out_specs=specs(vmem)[0],
        scratch_shapes=[pltpu.VMEM((CTX, 2 * HD), jnp.bfloat16)],
        compiler_params=pltpu.CompilerParams(vmem_limit_bytes=VMEM),
        name="decode",
    )(inst, partner, slots, lens, queries, fresh, context, *came)


BLOCK = 128


def prefill_kernel(arrived_ref, mask_ref, out_ref, packed_ref, keys_ref, last_ref):
    size = N_TP * MESSAGE
    to, src = iota((size, size), 0), iota((size, size), 1)
    order = (
        (to // 16 == src // 2 % TILES) & (to // 2 % 8 == src // MESSAGE) & (to % 2 == src % 2)
    )
    order = order.astype(jnp.float32).astype(jnp.bfloat16)
    for i in range(0, N_INST, 8):
        rows = jnp.concatenate(
            [arrived_ref[(i + j) * size : (i + j + 1) * size, :] for j in range(8)], axis=1
        )
        rows = dot(order, rows).astype(jnp.bfloat16)
        for tile in range(TILES):
            for j in range(8):
                packed_ref[tile, (i + j) * 16 : (i + j + 1) * 16, :] = rows[
                    tile * 16 : (tile + 1) * 16, j * LANES : (j + 1) * LANES
                ]
    mask = mask_ref[...].astype(jnp.float32)
    late = iota((SLOTS, BLOCK), 0) % BLOCK > iota((SLOTS, BLOCK), 1)
    keys_ref[:, :HD] = packed_ref[GROUP]
    keys_ref[:, HD:] = mask_ref[...]
    last_ref[:, :HD] = packed_ref[GROUP]
    last_ref[:, HD:] = jnp.where(late, MASKED, mask).astype(jnp.bfloat16)
    position = iota((BLOCK, BLOCK), 0) == iota((BLOCK, BLOCK), 1)
    position = position.astype(jnp.float32).astype(jnp.bfloat16)
    positions = jnp.concatenate([position] * GROUP, axis=0)
    for start in range(0, SLOTS, BLOCK):
        end = start + BLOCK
        filled = (mask_ref[start:end, 0:1].astype(jnp.float32) == 0).astype(jnp.float32)
        filled = jnp.concatenate([filled] * GROUP, axis=0)
        query = jnp.concatenate([packed_ref[h, start:end, :] for h in range(GROUP)], axis=0)
        query = jnp.concatenate([query, positions], axis=1)
        scores = dot(query, last_ref[start:end, :], NT)
        if start:
            scores = jnp.concatenate([dot(query, keys_ref[:start, :], NT), scores], axis=1)
        top = jnp.max(scores, axis=1, keepdims=True)
        expo = jnp.exp2((scores - top) * LOG2_SCALE).astype(jnp.bfloat16)
        ones = jnp.ones((end, LANES), jnp.bfloat16)
        out = dot(expo, jnp.concatenate([packed_ref[GROUP + 1, :end, :], ones], axis=1))
        out = (out[:, :HD] * (filled / out[:, HD:])).astype(jnp.bfloat16)
        for h in range(GROUP):
            out_ref[start:end, h * HD : (h + 1) * HD] = out[h * BLOCK : (h + 1) * BLOCK]


def prefill(arrived, mask):
    vmem = pltpu.VMEM
    return pl.pallas_call(
        prefill_kernel,
        out_shape=jax.ShapeDtypeStruct((SLOTS, GROUP * HD), jnp.bfloat16),
        in_specs=specs(vmem, vmem),
        out_specs=specs(vmem)[0],
        scratch_shapes=[
            pltpu.VMEM((TILES, SLOTS, LANES), jnp.bfloat16),
            pltpu.VMEM((SLOTS, 2 * HD), jnp.bfloat16),
            pltpu.VMEM((SLOTS, 2 * HD), jnp.bfloat16),
        ],
        compiler_params=pltpu.CompilerParams(vmem_limit_bytes=VMEM),
        name="prefill",
    )(arrived, mask)


def local(
    step_queries,
    step_keyvals,
    cache_pages,
    block_table,
    context_len,
    partner,
    moved_slot,
    prompt_queries,
    prompt_keyvals,
    prompt_target,
):
    inst = lax.axis_index("inst")
    device = inst * N_TP + lax.axis_index("tp")
    targets = prompt_target.reshape(-1, LANES)
    sent = dispatch(
        device[None], targets, prompt_queries, prompt_keyvals.reshape(ROWS_DEV * KVH, 2 * HD)
    )
    arrived = lax.all_to_all(
        sent.reshape(N_INST * N_TP, MESSAGE // 4, 4, LANES), ("inst", "tp"), 0, 0, tiled=True
    ).reshape(sent.shape)

    cache = cache_pages.reshape(POOL * PAGE, 2 * HD)
    leaving, context, mask = prepare(inst[None], moved_slot, block_table, cache, targets)
    came = [
        lax.ppermute(leaving, "inst", [(i, i ^ 1 << bit) for i in range(N_INST)])
        for bit in range(BITS)
    ]
    prefill_output = prefill(arrived, mask)
    step_queries, prefill_output = lax.optimization_barrier((step_queries, prefill_output))
    decode_output = decode(
        inst[None], partner, moved_slot, context_len,
        step_queries.reshape(STEPS * REQ, GROUP * HD),
        step_keyvals.reshape(STEPS * REQ, 2 * HD), context, came,
    )
    return decode_output.reshape(step_queries.shape), prefill_output


def solution(mesh):
    placed = (
        P(None, "inst", "tp"),
        P(None, "inst", "tp", None),
        P("inst", None, "tp", None),
        P("inst", None),
        P(),
        P(),
        P(),
        P(("inst", "tp"), None),
        P(("inst", "tp"), None, None),
        P(),
    )
    return jax.shard_map(
        local,
        mesh=mesh,
        in_specs=placed,
        out_specs=(P(None, "inst", "tp"), P("inst", "tp")),
        check_vma=False,
    )
```

time: 152 us -> 114 us (0.75)
  the two profiles are of different devices: /device:TPU:16 before, /device:TPU:1 now
where the time goes in v2:
time: 114 us; the launch traced here: 112 us
  starting transfers between devices  50.9 us (45%)
  waiting for transfers between devices  36.7 us (32%)
  Pallas kernels  21.3 us (19%)
  local copies, waits for them, and re-layouts  2.22 us (2%)
    ppermute x6, waiting for transfers between devices, local(): lax.ppermute(leaving, 'inst', [(i, i ^ 1 << bit) for i in range(N_INST)])  36.7 us
    ppermute x6, starting transfers between devices, local(): lax.ppermute(leaving, 'inst', [(i, i ^ 1 << bit) for i in range(N_INST)])  28.7 us
    all_to_all x1, starting transfers between devices, local(): lax.all_to_all(sent.reshape(N_INST * N_TP, MESSAGE // 4, 4, LANES), ('ins...  22.2 us
    pallas_call x1, Pallas kernels, prefill(): pl.pallas_call(prefill_kernel, out_shape=jax.ShapeDtypeStruct((SLOTS, GRO...  10.5 us
    pallas_call x1, Pallas kernels, dispatch(): pl.pallas_call(dispatch_kernel, out_shape=pltpu.HBM((rows, LANES), jnp.bf...  6.4 us
    pallas_call x1, Pallas kernels, decode(): pl.pallas_call(decode_kernel, out_shape=jax.ShapeDtypeStruct(queries.shap...  2.65 us
  transfers between devices with their start and end apart: 7, of which 1 were waited for; matrix products, arithmetic and copies ran while one was open for 0% of the time, Pallas kernels for 11%

profile of v2, /device:TPU:1, one launch (start us, length us, event | category | flops | bytes accessed | tf_op | source)
XLA Modules:
  0.0 112.0 jit_solution(3622278161971241159)
XLA Ops:
  0.6 6.4 %dispatch.1 = bf16[10240,128]{1,0:T(8,128)(2,1)} custom-call(s32[1]{0:T(128)} %bitcast.1.me_ref, s32[256,128]{1,0:T(8,128)} %bitcast.12, bf16[64,8192]{1,0:T(8,128)(2,1)} %queries_ref.1, bf16[512,256]{1,0:T(8,128)(2,1)} %bitcast.17), custom_call_target="tpu_custom_call" | custom-call | tf_op jit(solution)/shard_map/dispatch/pallas_call | solution.py:90
  7.0 0.0 copy-start.3
  7.0 0.0 copy-start.6
  7.0 0.0 copy-start.8
  7.0 22.2 %all-to-all-start = ((bf16[512,5,4,128]{3,2,1,0:T(4,128)(2,1)}), bf16[512,5,4,128]{3,2,1,0:T(4,128)(2,1)S(1)}, u32[]{:S(2)}, u32[]{:S(2)}) async-start(bf16[512,5,4,128]{3,2,1,0:T(4,128)(2,1)} %bitcast.16), calls=%async_computation | async-start | bytes 5242880 | tf_op jit(solution)/shard_map/all_to_all | solution.py:299
  29.2 0.0 copy-done.3
  29.2 0.0 copy-done.6
  29.2 0.0 copy-done.8
  29.2 0.0 copy-start.2
  29.3 1.2 %copy-done.2 = bf16[128,16,1,256]{3,1,2,0:T(8,128)(2,1)S(1)} copy-done((bf16[128,16,1,256]{3,1,2,0:T(8,128)(2,1)S(1)}, bf16[128,16,1,256]{3,1,2,0:T(8,128)(2,1)}, u32[]{:S(2)}) %copy-start.2) | copy-done | bytes 1048600
  30.5 1.8 %prepare.1 = (bf16[256,256]{1,0:T(8,128)(2,1)}, bf16[2048,256]{1,0:T(8,128)(2,1)S(1)}, bf16[1024,128]{1,0:T(8,128)(2,1)S(1)}) custom-call(s32[1]{0:T(128)} %bitcast.inst_ref, s32[64]{0:T(128)S(1)} %copy-done.8, s32[8,16]{1,0:T(8,128)S(1)} %copy-done.6, bf16[2048,256]{1,0:T(8,128)(2,1)S(1)} %bitcast.11, s32[256,128]{1,0:T(8,128)S(1)} %bitcast.13), custom_call_target="tpu_custom_call" | custom-call | tf_op jit(solution)/shard_map/prepare/pallas_call | solution.py:140
  32.3 0.0 copy-start
  32.3 1.0 copy-done
  33.2 0.0 copy-start.5
  33.2 3.4 %collective-permute-start = (bf16[256,256]{1,0:T(8,128)(2,1)}, bf16[256,256]{1,0:T(8,128)(2,1)S(1)}, u32[]{:S(2)}, u32[]{:S(2)}) collective-permute-start(bf16[256,256]{1,0:T(8,128)(2,1)} %get-tuple-element.10), channel_id=1, source_target_pairs={{0,8},{8,0},{16,24},{24,16},{32,40},{40,32},{48,56},{56,48},{64,72... | collective-permute-start | bytes 393224 | tf_op jit(solution)/shard_map/ppermute | solution.py:306
  36.7 4.0 %collective-permute-start.1 = (bf16[256,256]{1,0:T(8,128)(2,1)}, bf16[256,256]{1,0:T(8,128)(2,1)S(1)}, u32[]{:S(2)}, u32[]{:S(2)}) collective-permute-start(bf16[256,256]{1,0:T(8,128)(2,1)} %get-tuple-element.10), channel_id=1, source_target_pairs={{0,16},{8,24},{16,0},{24,8},{32,48},{40,56},{48,32},{56,40},{64,80... | collective-permute-start | bytes 393224 | tf_op jit(solution)/shard_map/ppermute | solution.py:306
  40.7 4.6 %collective-permute-start.2 = (bf16[256,256]{1,0:T(8,128)(2,1)}, bf16[256,256]{1,0:T(8,128)(2,1)S(1)}, u32[]{:S(2)}, u32[]{:S(2)}) collective-permute-start(bf16[256,256]{1,0:T(8,128)(2,1)} %get-tuple-element.10), channel_id=1, source_target_pairs={{0,32},{8,40},{16,48},{24,56},{32,0},{40,8},{48,16},{56,24},{64,96... | collective-permute-start | bytes 393224 | tf_op jit(solution)/shard_map/ppermute | solution.py:306
  45.3 3.1 %collective-permute-start.3 = (bf16[256,256]{1,0:T(8,128)(2,1)}, bf16[256,256]{1,0:T(8,128)(2,1)S(1)}, u32[]{:S(2)}, u32[]{:S(2)}) collective-permute-start(bf16[256,256]{1,0:T(8,128)(2,1)} %get-tuple-element.10), channel_id=1, source_target_pairs={{0,64},{8,72},{16,80},{24,88},{32,96},{40,104},{48,112},{56,120},{... | collective-permute-start | bytes 393224 | tf_op jit(solution)/shard_map/ppermute | solution.py:306
  48.4 4.3 %collective-permute-start.4 = (bf16[256,256]{1,0:T(8,128)(2,1)}, bf16[256,256]{1,0:T(8,128)(2,1)S(1)}, u32[]{:S(2)}, u32[]{:S(2)}) collective-permute-start(bf16[256,256]{1,0:T(8,128)(2,1)} %get-tuple-element.10), channel_id=1, source_target_pairs={{0,128},{8,136},{16,144},{24,152},{32,160},{40,168},{48,176},{56,1... | collective-permute-start | bytes 393224 | tf_op jit(solution)/shard_map/ppermute | solution.py:306
  52.7 36.7 %collective-permute-done.refs_0_ = bf16[256,256]{1,0:T(8,128)(2,1)S(1)} collective-permute-done((bf16[256,256]{1,0:T(8,128)(2,1)}, bf16[256,256]{1,0:T(8,128)(2,1)S(1)}, u32[]{:S(2)}, u32[]{:S(2)}) %collective-permute-start) | collective-permute-done | bytes 131104 | tf_op jit(solution)/shard_map/ppermute | solution.py:306
  89.5 9.2 %collective-permute-start.5 = (bf16[256,256]{1,0:T(8,128)(2,1)}, bf16[256,256]{1,0:T(8,128)(2,1)}, u32[]{:S(2)}, u32[]{:S(2)}) collective-permute-start(bf16[256,256]{1,0:T(8,128)(2,1)} %get-tuple-element.10), channel_id=1, source_target_pairs={{0,256},{8,264},{16,272},{24,280},{32,288},{40,296},{48,304},{56,3... | collective-permute-start | bytes 393224 | tf_op jit(solution)/shard_map/ppermute | solution.py:306
  98.7 0.0 all-to-all-done
  98.7 0.0 copy-start.1
  98.7 0.0 copy-start.4
  98.8 0.0 copy-start.7
  98.8 0.0 copy-start.9
  98.8 0.0 copy-start.10
  98.8 10.5 %prefill.1 = bf16[1024,1024]{1,0:T(8,128)(2,1)} custom-call(bf16[10240,128]{1,0:T(8,128)(2,1)S(1)} %bitcast.10, bf16[1024,128]{1,0:T(8,128)(2,1)S(1)} %get-tuple-element.7.mask_ref), custom_call_target="tpu_custom_call" | custom-call | tf_op jit(solution)/shard_map/prefill/pallas_call | solution.py:266
  109.2 0.0 collective-permute-done.1.refs_1_
  109.3 0.0 collective-permute-done.2.refs_2_
  109.3 0.0 collective-permute-done.3.refs_3_
  109.3 0.0 collective-permute-done.4.refs_4_
  109.3 0.0 collective-permute-done.5.refs_5_
  109.3 0.0 copy-done.5
  109.3 0.0 copy-done.1
  109.3 0.0 copy-done.4
  109.3 0.0 copy-done.7
  109.3 0.0 copy-done.9
  109.3 0.0 copy-done.10
  109.3 2.7 %decode.1 = bf16[32,1024]{1,0:T(8,128)(2,1)} custom-call(s32[1]{0:T(128)} %bitcast.inst_ref, s32[64]{0:T(128)S(1)} %copy-done.10, s32[64]{0:T(128)S(1)} %copy-done.9, s32[512]{0:T(512)S(1)} %copy-done.7, bf16[32,1024]{1,0:T(8,128)(2,1)S(1)} %bitcast.14, bf16[32,256]{1,0:T(8,128)(2,1)S(1)} %bitcast.15, bf16[2048,256]{1,0:T(8,128)(2,1)S(1)} %copy-done.1, ...), custom_call_target="tpu_custom_call" | custom-call | tf_op jit(solution)/shard_map/decode/pallas_call | solution.py:206
Async XLA Ops:
  7.0 22.2 %copy-start.3 = (s32[32768,1]{0,1:T(1,128)S(1)}, s32[32768,1]{0,1:T(1,128)}, u32[]{:S(2)}) copy-start(s32[32768,1]{0,1:T(1,128)} %param.19) | copy-start | bytes 393220
  7.0 22.2 %copy-start.6 = (s32[8,16]{1,0:T(8,128)S(1)}, s32[8,16]{1,0:T(8,128)}, u32[]{:S(2)}) copy-start(s32[8,16]{1,0:T(8,128)} %table_ref.1) | copy-start | bytes 1540
  7.0 22.2 %copy-start.8 = (s32[64]{0:T(128)S(1)}, s32[64]{0:T(128)}, u32[]{:S(2)}) copy-start(s32[64]{0:T(128)} %slot_ref.3) | copy-start | bytes 772
  7.0 91.7 %all-to-all-start = ((bf16[512,5,4,128]{3,2,1,0:T(4,128)(2,1)}), bf16[512,5,4,128]{3,2,1,0:T(4,128)(2,1)S(1)}, u32[]{:S(2)}, u32[]{:S(2)}) async-start(bf16[512,5,4,128]{3,2,1,0:T(4,128)(2,1)} %bitcast.16), calls=%async_computation | async-start | bytes 5242880 | tf_op jit(solution)/shard_map/all_to_all | solution.py:299
  29.2 1.2 %copy-start.2 = (bf16[128,16,1,256]{3,1,2,0:T(8,128)(2,1)S(1)}, bf16[128,16,1,256]{3,1,2,0:T(8,128)(2,1)}, u32[]{:S(2)}) copy-start(bf16[128,16,1,256]{3,1,2,0:T(8,128)(2,1)} %param.12) | copy-start | bytes 3145732
  32.3 1.0 copy-start
  33.2 76.1 %copy-start.5 = (bf16[4,8,1,256]{3,1,2,0:T(8,128)(2,1)S(1)}, bf16[4,8,1,256]{3,1,2,0:T(8,128)(2,1)}, u32[]{:S(2)}) copy-start(bf16[4,8,1,256]{3,1,2,0:T(8,128)(2,1)} %param.11) | copy-start | bytes 49156
  33.2 56.2 %collective-permute-start = (bf16[256,256]{1,0:T(8,128)(2,1)}, bf16[256,256]{1,0:T(8,128)(2,1)S(1)}, u32[]{:S(2)}, u32[]{:S(2)}) collective-permute-start(bf16[256,256]{1,0:T(8,128)(2,1)} %get-tuple-element.10), channel_id=1, source_target_pairs={{0,8},{8,0},{16,24},{24,16},{32,40},{40,32},{48,56},{56,48},{64,72... | collective-permute-start | bytes 393224 | tf_op jit(solution)/shard_map/ppermute | solution.py:306
  36.7 72.6 %collective-permute-start.1 = (bf16[256,256]{1,0:T(8,128)(2,1)}, bf16[256,256]{1,0:T(8,128)(2,1)S(1)}, u32[]{:S(2)}, u32[]{:S(2)}) collective-permute-start(bf16[256,256]{1,0:T(8,128)(2,1)} %get-tuple-element.10), channel_id=1, source_target_pairs={{0,16},{8,24},{16,0},{24,8},{32,48},{40,56},{48,32},{56,40},{64,80... | collective-permute-start | bytes 393224 | tf_op jit(solution)/shard_map/ppermute | solution.py:306
  40.7 68.5 %collective-permute-start.2 = (bf16[256,256]{1,0:T(8,128)(2,1)}, bf16[256,256]{1,0:T(8,128)(2,1)S(1)}, u32[]{:S(2)}, u32[]{:S(2)}) collective-permute-start(bf16[256,256]{1,0:T(8,128)(2,1)} %get-tuple-element.10), channel_id=1, source_target_pairs={{0,32},{8,40},{16,48},{24,56},{32,0},{40,8},{48,16},{56,24},{64,96... | collective-permute-start | bytes 393224 | tf_op jit(solution)/shard_map/ppermute | solution.py:306
  45.3 64.0 %collective-permute-start.3 = (bf16[256,256]{1,0:T(8,128)(2,1)}, bf16[256,256]{1,0:T(8,128)(2,1)S(1)}, u32[]{:S(2)}, u32[]{:S(2)}) collective-permute-start(bf16[256,256]{1,0:T(8,128)(2,1)} %get-tuple-element.10), channel_id=1, source_target_pairs={{0,64},{8,72},{16,80},{24,88},{32,96},{40,104},{48,112},{56,120},{... | collective-permute-start | bytes 393224 | tf_op jit(solution)/shard_map/ppermute | solution.py:306
  48.4 60.9 %collective-permute-start.4 = (bf16[256,256]{1,0:T(8,128)(2,1)}, bf16[256,256]{1,0:T(8,128)(2,1)S(1)}, u32[]{:S(2)}, u32[]{:S(2)}) collective-permute-start(bf16[256,256]{1,0:T(8,128)(2,1)} %get-tuple-element.10), channel_id=1, source_target_pairs={{0,128},{8,136},{16,144},{24,152},{32,160},{40,168},{48,176},{56,1... | collective-permute-start | bytes 393224 | tf_op jit(solution)/shard_map/ppermute | solution.py:306
  89.5 19.8 %collective-permute-start.5 = (bf16[256,256]{1,0:T(8,128)(2,1)}, bf16[256,256]{1,0:T(8,128)(2,1)}, u32[]{:S(2)}, u32[]{:S(2)}) collective-permute-start(bf16[256,256]{1,0:T(8,128)(2,1)} %get-tuple-element.10), channel_id=1, source_target_pairs={{0,256},{8,264},{16,272},{24,280},{32,288},{40,296},{48,304},{56,3... | collective-permute-start | bytes 393224 | tf_op jit(solution)/shard_map/ppermute | solution.py:306
  98.7 10.6 %copy-start.1 = (bf16[2048,256]{1,0:T(8,128)(2,1)S(1)}, bf16[2048,256]{1,0:T(8,128)(2,1)}, u32[]{:S(2)}) copy-start(bf16[2048,256]{1,0:T(8,128)(2,1)} %copy-done) | copy-start | bytes 3145732
  98.7 10.6 %copy-start.4 = (bf16[4,8,1024]{2,1,0:T(8,128)(2,1)S(1)}, bf16[4,8,1024]{2,1,0:T(8,128)(2,1)}, u32[]{:S(2)}) copy-start(bf16[4,8,1024]{2,1,0:T(8,128)(2,1)} %param.10) | copy-start | bytes 196612
  98.8 10.6 %copy-start.7 = (s32[512]{0:T(512)S(1)}, s32[512]{0:T(512)}, u32[]{:S(2)}) copy-start(s32[512]{0:T(512)} %lens_ref.1) | copy-start | bytes 6148
  98.8 10.6 %copy-start.9 = (s32[64]{0:T(128)S(1)}, s32[64]{0:T(128)}, u32[]{:S(2)}) copy-start(s32[64]{0:T(128)} %slot_ref.3) | copy-start | bytes 772
  98.8 10.6 %copy-start.10 = (s32[64]{0:T(128)S(1)}, s32[64]{0:T(128)}, u32[]{:S(2)}) copy-start(s32[64]{0:T(128)} %partner_ref.1) | copy-start | bytes 772

commit v3 on v2

--- a/solution.py
+++ b/solution.py
@@ -32,7 +32,7 @@
 NT = ((1,), (1,))
 
 
-INSTS = 8
+INSTS = 32
 
 
 def dispatch_kernel(me_ref, target_ref, queries_ref, keyvals_ref, out_ref, place_ref, rows_ref):
@@ -72,9 +72,9 @@
             to, col = c % 8, c // 8
             rows_ref[to * ROWS_DEV : (to + 1) * ROWS_DEV, col * LANES : (col + 1) * LANES] = piece
 
-    down, along = iota((LANES, 512), 0), iota((LANES, 512), 1)
+    down, along = iota((INSTS * 16, 512), 0), iota((INSTS * 16, 512), 1)
     wanted = (step * INSTS + down // 16) * CAP + down % 2
-    place = jnp.broadcast_to(place_ref[0:1, :], (LANES, 512))
+    place = jnp.broadcast_to(place_ref[0:1, :], (INSTS * 16, 512))
     chosen = (place == wanted) & (along // ROWS_DEV == down // 2 % 8)
     out = dot(chosen.astype(jnp.float32).astype(jnp.bfloat16), rows_ref[...])
     out = out.astype(jnp.bfloat16)
@@ -151,24 +151,10 @@
     )(inst, slots, table, cache, targets)
 
 
-BITS = N_INST.bit_length() - 1
-
-
-def decode_kernel(
-    inst_ref, partner_ref, slot_ref, lens_ref, queries_ref, fresh_ref, context_ref, *refs
-):
-    *came_refs, out_ref, came_ref = refs
+def decode_kernel(inst_ref, lens_ref, queries_ref, fresh_ref, context_ref, out_ref):
     inst = inst_ref[0]
-    other = partner_ref[inst]
-    moved = slot_ref[inst]
-    for bit in range(BITS):
-
-        @pl.when(jnp.bitwise_xor(inst, other) == 1 << bit)
-        def _(bit=bit):
-            came_ref[...] = came_refs[bit][...]
-
     rows = STEPS * REQ
-    queries, fresh, came = queries_ref[...], fresh_ref[...], came_ref[...]
+    queries, fresh = queries_ref[...], fresh_ref[...]
     query = jnp.concatenate([queries[:, g * HD : (g + 1) * HD] for g in range(GROUP)], axis=0)
     n = GROUP * rows
     row = iota((n, 1), 0)
@@ -178,87 +164,153 @@
     newer = jnp.where((along % REQ == request) & (along // REQ <= moment), newer, MASKED)
     past = jnp.zeros((n, CTX), jnp.float32)
     length = jnp.zeros((n, 1), jnp.int32)
-    values = []
     for r in range(REQ):
-        context = jnp.where(moved == r, came, context_ref[r * CTX : (r + 1) * CTX, :])
-        values.append(context[:, HD:])
-        past = jnp.where(request == r, dot(query, context[:, :HD], NT), past)
-        source = jnp.where(moved == r, other * REQ + slot_ref[other], inst * REQ + r)
-        length = jnp.where(request == r, lens_ref[source], length)
+        keys = context_ref[r * CTX : (r + 1) * CTX, :HD]
+        past = jnp.where(request == r, dot(query, keys, NT), past)
+        length = jnp.where(request == r, lens_ref[inst * REQ + r], length)
     past = jnp.where(iota((n, CTX), 1) < length, past, MASKED)
+    past, newer = shares(past, newer)
+    out = dot(newer.astype(jnp.bfloat16), fresh[:, HD:])
+    for r in range(REQ):
+        weights = jnp.where(request == r, past, 0.0).astype(jnp.bfloat16)
+        out = out + dot(weights, context_ref[r * CTX : (r + 1) * CTX, HD:])
+    for g in range(GROUP):
+        out_ref[:, g * HD : (g + 1) * HD] = out[g * rows : (g + 1) * rows].astype(jnp.bfloat16)
+
+
+def shares(past, newer):
     top = jnp.maximum(
         jnp.max(past, axis=1, keepdims=True), jnp.max(newer, axis=1, keepdims=True)
     )
     past = jnp.exp2((past - top) * LOG2_SCALE)
     newer = jnp.exp2((newer - top) * LOG2_SCALE)
     total = jnp.sum(past, axis=1, keepdims=True) + jnp.sum(newer, axis=1, keepdims=True)
-    past, newer = past / total, newer / total
-    out = dot(newer.astype(jnp.bfloat16), fresh[:, HD:])
-    for r in range(REQ):
-        weights = jnp.where(request == r, past, 0.0).astype(jnp.bfloat16)
-        out = out + dot(weights, values[r])
-    for g in range(GROUP):
-        out_ref[:, g * HD : (g + 1) * HD] = out[g * rows : (g + 1) * rows].astype(jnp.bfloat16)
-
-
-def decode(inst, partner, slots, lens, queries, fresh, context, came):
+    return past / total, newer / total
+
+
+def decode(inst, lens, queries, fresh, context):
     smem, vmem = pltpu.SMEM, pltpu.VMEM
     return pl.pallas_call(
         decode_kernel,
+        out_shape=jax.ShapeDtypeStruct(queries.shape, jnp.bfloat16),
+        in_specs=specs(smem, smem, vmem, vmem, vmem),
+        out_specs=specs(vmem)[0],
+        compiler_params=pltpu.CompilerParams(vmem_limit_bytes=VMEM),
+        name="decode",
+    )(inst, lens, queries, fresh, context)
+
+
+BITS = N_INST.bit_length() - 1
+
+
+def traded_kernel(
+    inst_ref, partner_ref, slot_ref, lens_ref, queries_ref, fresh_ref, decoded_ref, *refs
+):
+    *came_refs, out_ref = refs
+    inst = inst_ref[0]
+    other = partner_ref[inst]
+    moved = slot_ref[inst]
+    distance = jnp.bitwise_xor(inst, other)
+    came = came_refs[0][...]
+    for bit in range(1, BITS):
+        came = jnp.where(distance == 1 << bit, came_refs[bit][...], came)
+    rows = STEPS * REQ
+    chosen = iota((8, rows), 1) == iota((8, rows), 0) * REQ + moved
+    chosen = chosen.astype(jnp.float32).astype(jnp.bfloat16)
+    queries = dot(chosen, queries_ref[...])
+    fresh = dot(chosen, fresh_ref[...]).astype(jnp.bfloat16)
+    query = jnp.concatenate([queries[:, g * HD : (g + 1) * HD] for g in range(GROUP)], axis=0)
+    query = query.astype(jnp.bfloat16)
+    n = GROUP * 8
+    newer = dot(query, fresh[:, :HD], NT)
+    moment, along = iota((n, 8), 0) % 8, iota((n, 8), 1)
+    newer = jnp.where((along <= moment) & (along < STEPS), newer, MASKED)
+    length = lens_ref[other * REQ + slot_ref[other]]
+    past = jnp.where(iota((n, CTX), 1) < length, dot(query, came[:, :HD], NT), MASKED)
+    past, newer = shares(past, newer)
+    out = dot(past.astype(jnp.bfloat16), came[:, HD:])
+    out = out + dot(newer.astype(jnp.bfloat16), fresh[:, HD:])
+    out = jnp.concatenate([out[g * 8 : (g + 1) * 8] for g in range(GROUP)], axis=1)
+    out = dot(chosen, out.astype(jnp.bfloat16), ((0,), (0,)))
+    here = iota((rows, 1), 0) % REQ == moved
+    out_ref[...] = jnp.where(here, out, decoded_ref[...].astype(jnp.float32)).astype(jnp.bfloat16)
+
+
+def traded(inst, partner, slots, lens, queries, fresh, decoded, came):
+    smem, vmem = pltpu.SMEM, pltpu.VMEM
+    return pl.pallas_call(
+        traded_kernel,
         out_shape=jax.ShapeDtypeStruct(queries.shape, jnp.bfloat16),
         in_specs=specs(*[smem] * 4, *[vmem] * (3 + BITS)),
         out_specs=specs(vmem)[0],
-        scratch_shapes=[pltpu.VMEM((CTX, 2 * HD), jnp.bfloat16)],
-        compiler_params=pltpu.CompilerParams(vmem_limit_bytes=VMEM),
-        name="decode",
-    )(inst, partner, slots, lens, queries, fresh, context, *came)
+        compiler_params=pltpu.CompilerParams(vmem_limit_bytes=VMEM),
+        name="traded",
+    )(inst, partner, slots, lens, queries, fresh, decoded, *came)
 
 
 BLOCK = 128
-
-
-def prefill_kernel(arrived_ref, mask_ref, out_ref, packed_ref, keys_ref, last_ref):
+HEADS = 4
+
+
+def prefill_kernel(arrived_ref, mask_ref, out_ref, packed_ref, keys_ref, last_ref, values_ref):
     size = N_TP * MESSAGE
     to, src = iota((size, size), 0), iota((size, size), 1)
     order = (
         (to // 16 == src // 2 % TILES) & (to // 2 % 8 == src // MESSAGE) & (to % 2 == src % 2)
     )
     order = order.astype(jnp.float32).astype(jnp.bfloat16)
-    for i in range(0, N_INST, 8):
+    late = iota((BLOCK, BLOCK), 0) > iota((BLOCK, BLOCK), 1)
+    position = iota((BLOCK, BLOCK), 0) == iota((BLOCK, BLOCK), 1)
+    position = position.astype(jnp.float32).astype(jnp.bfloat16)
+    positions = jnp.concatenate([position] * HEADS, axis=0)
+
+    def bring(start, end):
+        first = start // 16
         rows = jnp.concatenate(
-            [arrived_ref[(i + j) * size : (i + j + 1) * size, :] for j in range(8)], axis=1
+            [arrived_ref[(first + j) * size : (first + j + 1) * size, :] for j in range(8)], axis=1
         )
         rows = dot(order, rows).astype(jnp.bfloat16)
         for tile in range(TILES):
             for j in range(8):
-                packed_ref[tile, (i + j) * 16 : (i + j + 1) * 16, :] = rows[
+                packed_ref[tile, start + j * 16 : start + (j + 1) * 16, :] = rows[
                     tile * 16 : (tile + 1) * 16, j * LANES : (j + 1) * LANES
                 ]
-    mask = mask_ref[...].astype(jnp.float32)
-    late = iota((SLOTS, BLOCK), 0) % BLOCK > iota((SLOTS, BLOCK), 1)
-    keys_ref[:, :HD] = packed_ref[GROUP]
-    keys_ref[:, HD:] = mask_ref[...]
-    last_ref[:, :HD] = packed_ref[GROUP]
-    last_ref[:, HD:] = jnp.where(late, MASKED, mask).astype(jnp.bfloat16)
-    position = iota((BLOCK, BLOCK), 0) == iota((BLOCK, BLOCK), 1)
-    position = position.astype(jnp.float32).astype(jnp.bfloat16)
-    positions = jnp.concatenate([position] * GROUP, axis=0)
-    for start in range(0, SLOTS, BLOCK):
-        end = start + BLOCK
-        filled = (mask_ref[start:end, 0:1].astype(jnp.float32) == 0).astype(jnp.float32)
-        filled = jnp.concatenate([filled] * GROUP, axis=0)
-        query = jnp.concatenate([packed_ref[h, start:end, :] for h in range(GROUP)], axis=0)
+        mask = mask_ref[start:end, :]
+        keys_ref[start:end, :HD] = packed_ref[GROUP, start:end, :]
+        keys_ref[start:end, HD:] = mask
+        last_ref[start:end, :HD] = packed_ref[GROUP, start:end, :]
+        mask = jnp.where(late, MASKED, mask.astype(jnp.float32))
+        last_ref[start:end, HD:] = mask.astype(jnp.bfloat16)
+        values_ref[start:end, :HD] = packed_ref[GROUP + 1, start:end, :]
+        values_ref[start:end, HD:] = jnp.ones((BLOCK, LANES), jnp.bfloat16)
+
+    def scored(start, end, heads):
+        if heads[0] == 0:
+            bring(start, end)
+        query = jnp.concatenate([packed_ref[h, start:end, :] for h in heads], axis=0)
         query = jnp.concatenate([query, positions], axis=1)
         scores = dot(query, last_ref[start:end, :], NT)
         if start:
             scores = jnp.concatenate([dot(query, keys_ref[:start, :], NT), scores], axis=1)
+        return scores
+
+    work = [
+        (start, start + BLOCK, range(h, h + HEADS))
+        for start in range(0, SLOTS, BLOCK)
+        for h in range(0, GROUP, HEADS)
+    ]
+    scores = scored(*work[0])
+    for i, (start, end, heads) in enumerate(work):
+        ahead = scored(*work[i + 1]) if i + 1 < len(work) else None
+        filled = (mask_ref[start:end, 0:1].astype(jnp.float32) == 0).astype(jnp.float32)
+        filled = jnp.concatenate([filled] * HEADS, axis=0)
         top = jnp.max(scores, axis=1, keepdims=True)
         expo = jnp.exp2((scores - top) * LOG2_SCALE).astype(jnp.bfloat16)
-        ones = jnp.ones((end, LANES), jnp.bfloat16)
-        out = dot(expo, jnp.concatenate([packed_ref[GROUP + 1, :end, :], ones], axis=1))
+        out = dot(expo, values_ref[:end, :])
         out = (out[:, :HD] * (filled / out[:, HD:])).astype(jnp.bfloat16)
-        for h in range(GROUP):
-            out_ref[start:end, h * HD : (h + 1) * HD] = out[h * BLOCK : (h + 1) * BLOCK]
+        for j, h in enumerate(heads):
+            out_ref[start:end, h * HD : (h + 1) * HD] = out[j * BLOCK : (j + 1) * BLOCK]
+        scores = ahead
 
 
 def prefill(arrived, mask):
@@ -270,6 +322,7 @@
         out_specs=specs(vmem)[0],
         scratch_shapes=[
             pltpu.VMEM((TILES, SLOTS, LANES), jnp.bfloat16),
+            pltpu.VMEM((SLOTS, 2 * HD), jnp.bfloat16),
             pltpu.VMEM((SLOTS, 2 * HD), jnp.bfloat16),
             pltpu.VMEM((SLOTS, 2 * HD), jnp.bfloat16),
         ],
@@ -302,18 +355,18 @@
 
     cache = cache_pages.reshape(POOL * PAGE, 2 * HD)
     leaving, context, mask = prepare(inst[None], moved_slot, block_table, cache, targets)
+    queries = step_queries.reshape(STEPS * REQ, GROUP * HD)
+    fresh = step_keyvals.reshape(STEPS * REQ, 2 * HD)
+    decoded = decode(inst[None], context_len, queries, fresh, context)
+    leaving, decoded = lax.optimization_barrier((leaving, decoded))
     came = [
         lax.ppermute(leaving, "inst", [(i, i ^ 1 << bit) for i in range(N_INST)])
         for bit in range(BITS)
     ]
     prefill_output = prefill(arrived, mask)
-    step_queries, prefill_output = lax.optimization_barrier((step_queries, prefill_output))
-    decode_output = decode(
-        inst[None], partner, moved_slot, context_len,
-        step_queries.reshape(STEPS * REQ, GROUP * HD),
-        step_keyvals.reshape(STEPS * REQ, 2 * HD), context, came,
-    )
-    return decode_output.reshape(step_queries.shape), prefill_output
+    queries, prefill_output = lax.optimization_barrier((queries, prefill_output))
+    decoded = traded(inst[None], partner, moved_slot, context_len, queries, fresh, decoded, came)
+    return decoded.reshape(step_queries.shape), prefill_output
 
 
 def solution(mesh):

time: 114 us -> 111 us (0.974)
    pallas_call x0 -> x1, Pallas kernels: none -> 2.38 us  [traded(): pl.pallas_call(traded_kernel, out_shape=jax.ShapeDtypeStruct(queries.shap...]
    pallas_call x1, Pallas kernels: 6.4 us -> 4.61 us  [dispatch(): pl.pallas_call(dispatch_kernel, out_shape=pltpu.HBM((rows, LANES), jnp.bf...]
  transfers between devices with their start and end apart: 7 -> 7, of which waited for: 1 -> 1; matrix products, arithmetic and copies ran while one was open for 0% -> 0% of each run, Pallas kernels for 11% -> 12%
where the time goes in v3:
time: 111 us; the launch traced here: 109 us
  starting transfers between devices  50.8 us (46%)
  waiting for transfers between devices  36.2 us (33%)
  Pallas kernels  20.4 us (18%)
  local copies, waits for them, and re-layouts  1.25 us (1%)
    ppermute x6, waiting for transfers between devices, local(): lax.ppermute(leaving, 'inst', [(i, i ^ 1 << bit) for i in range(N_INST)])  36.2 us
    ppermute x6, starting transfers between devices, local(): lax.ppermute(leaving, 'inst', [(i, i ^ 1 << bit) for i in range(N_INST)])  28.6 us
    all_to_all x1, starting transfers between devices, local(): lax.all_to_all(sent.reshape(N_INST * N_TP, MESSAGE // 4, 4, LANES), ('ins...  22.2 us
    pallas_call x1, Pallas kernels, prefill(): pl.pallas_call(prefill_kernel, out_shape=jax.ShapeDtypeStruct((SLOTS, GRO...  10 us
    pallas_call x1, Pallas kernels, dispatch(): pl.pallas_call(dispatch_kernel, out_shape=pltpu.HBM((rows, LANES), jnp.bf...  4.61 us
    pallas_call x1, Pallas kernels, traded(): pl.pallas_call(traded_kernel, out_shape=jax.ShapeDtypeStruct(queries.shap...  2.38 us
  transfers between devices with their start and end apart: 7, of which 1 were waited for; matrix products, arithmetic and copies ran while one was open for 0% of the time, Pallas kernels for 12%

profile of v3, /device:TPU:1, one launch (start us, length us, event | category | flops | bytes accessed | tf_op | source)
XLA Modules:
  0.0 109.5 jit_solution(3374161262015837159)
XLA Ops:
  0.6 4.6 %dispatch.1 = bf16[10240,128]{1,0:T(8,128)(2,1)} custom-call(s32[1]{0:T(128)} %bitcast.2.me_ref, s32[256,128]{1,0:T(8,128)} %bitcast.12, bf16[64,8192]{1,0:T(8,128)(2,1)} %queries_ref.1, bf16[512,256]{1,0:T(8,128)(2,1)} %bitcast.19), custom_call_target="tpu_custom_call" | custom-call | tf_op jit(solution)/shard_map/dispatch/pallas_call | solution.py:90
  5.2 0.0 copy-start.1
  5.3 0.0 copy-start.5
  5.3 0.0 copy-start.6
  5.3 0.0 copy-start.2
  5.3 0.0 copy-start.3
  5.3 0.0 copy-start.4
  5.3 22.2 %all-to-all-start = ((bf16[512,5,4,128]{3,2,1,0:T(4,128)(2,1)}), bf16[512,5,4,128]{3,2,1,0:T(4,128)(2,1)S(1)}, u32[]{:S(2)}, u32[]{:S(2)}) async-start(bf16[512,5,4,128]{3,2,1,0:T(4,128)(2,1)} %bitcast.18), calls=%async_computation | async-start | bytes 5242880 | tf_op jit(solution)/shard_map/all_to_all | solution.py:352
  27.5 0.0 copy-done.1
  27.5 0.0 copy-done.5
  27.5 0.0 copy-done.6
  27.5 0.0 copy-start
  27.5 1.2 %copy-done = bf16[128,16,1,256]{3,1,2,0:T(8,128)(2,1)S(1)} copy-done((bf16[128,16,1,256]{3,1,2,0:T(8,128)(2,1)S(1)}, bf16[128,16,1,256]{3,1,2,0:T(8,128)(2,1)}, u32[]{:S(2)}) %copy-start) | copy-done | bytes 1048600
  28.7 1.8 %prepare.1 = (bf16[256,256]{1,0:T(8,128)(2,1)}, bf16[2048,256]{1,0:T(8,128)(2,1)S(1)}, bf16[1024,128]{1,0:T(8,128)(2,1)S(1)}) custom-call(s32[1]{0:T(128)} %bitcast.inst_ref, s32[64]{0:T(128)S(1)} %copy-done.6, s32[8,16]{1,0:T(8,128)S(1)} %copy-done.5, bf16[2048,256]{1,0:T(8,128)(2,1)S(1)} %bitcast.11, s32[256,128]{1,0:T(8,128)S(1)} %bitcast.13), custom_call_target="tpu_custom_call" | custom-call | tf_op jit(solution)/shard_map/prepare/pallas_call | solution.py:140
  30.5 0.0 copy-done.2
  30.5 0.0 copy-done.3
  30.5 0.0 copy-done.4
  30.5 1.6 %decode.1.decoded_ref = bf16[32,1024]{1,0:T(8,128)(2,1)S(1)} custom-call(s32[1]{0:T(128)} %bitcast.inst_ref, s32[512]{0:T(512)S(1)} %copy-done.4, bf16[32,1024]{1,0:T(8,128)(2,1)S(1)} %bitcast.14, bf16[32,256]{1,0:T(8,128)(2,1)S(1)} %bitcast.16, bf16[2048,256]{1,0:T(8,128)(2,1)S(1)} %get-tuple-element.12.context_ref), custom_call_target="tpu_custom_call" | custom-call | tf_op jit(solution)/shard_map/decode/pallas_call | solution.py:193
  32.1 0.0 copy-start.7
  32.2 3.3 %collective-permute-start = (bf16[256,256]{1,0:T(8,128)(2,1)}, bf16[256,256]{1,0:T(8,128)(2,1)S(1)}, u32[]{:S(2)}, u32[]{:S(2)}) collective-permute-start(bf16[256,256]{1,0:T(8,128)(2,1)} %get-tuple-element.14), channel_id=1, source_target_pairs={{0,8},{8,0},{16,24},{24,16},{32,40},{40,32},{48,56},{56,48},{64,72... | collective-permute-start | bytes 393224 | tf_op jit(solution)/shard_map/ppermute | solution.py:363
  35.5 4.0 %collective-permute-start.1 = (bf16[256,256]{1,0:T(8,128)(2,1)}, bf16[256,256]{1,0:T(8,128)(2,1)S(1)}, u32[]{:S(2)}, u32[]{:S(2)}) collective-permute-start(bf16[256,256]{1,0:T(8,128)(2,1)} %get-tuple-element.14), channel_id=1, source_target_pairs={{0,16},{8,24},{16,0},{24,8},{32,48},{40,56},{48,32},{56,40},{64,80... | collective-permute-start | bytes 393224 | tf_op jit(solution)/shard_map/ppermute | solution.py:363
  39.5 4.6 %collective-permute-start.2 = (bf16[256,256]{1,0:T(8,128)(2,1)}, bf16[256,256]{1,0:T(8,128)(2,1)S(1)}, u32[]{:S(2)}, u32[]{:S(2)}) collective-permute-start(bf16[256,256]{1,0:T(8,128)(2,1)} %get-tuple-element.14), channel_id=1, source_target_pairs={{0,32},{8,40},{16,48},{24,56},{32,0},{40,8},{48,16},{56,24},{64,96... | collective-permute-start | bytes 393224 | tf_op jit(solution)/shard_map/ppermute | solution.py:363
  44.1 3.1 %collective-permute-start.3 = (bf16[256,256]{1,0:T(8,128)(2,1)}, bf16[256,256]{1,0:T(8,128)(2,1)}, u32[]{:S(2)}, u32[]{:S(2)}) collective-permute-start(bf16[256,256]{1,0:T(8,128)(2,1)} %get-tuple-element.14), channel_id=1, source_target_pairs={{0,64},{8,72},{16,80},{24,88},{32,96},{40,104},{48,112},{56,120},{... | collective-permute-start | bytes 393224 | tf_op jit(solution)/shard_map/ppermute | solution.py:363
  47.2 4.3 %collective-permute-start.4 = (bf16[256,256]{1,0:T(8,128)(2,1)}, bf16[256,256]{1,0:T(8,128)(2,1)}, u32[]{:S(2)}, u32[]{:S(2)}) collective-permute-start(bf16[256,256]{1,0:T(8,128)(2,1)} %get-tuple-element.14), channel_id=1, source_target_pairs={{0,128},{8,136},{16,144},{24,152},{32,160},{40,168},{48,176},{56,1... | collective-permute-start | bytes 393224 | tf_op jit(solution)/shard_map/ppermute | solution.py:363
  51.6 36.2 %collective-permute-done.refs_0_ = bf16[256,256]{1,0:T(8,128)(2,1)S(1)} collective-permute-done((bf16[256,256]{1,0:T(8,128)(2,1)}, bf16[256,256]{1,0:T(8,128)(2,1)S(1)}, u32[]{:S(2)}, u32[]{:S(2)}) %collective-permute-start) | collective-permute-done | bytes 131104 | tf_op jit(solution)/shard_map/ppermute | solution.py:363
  87.7 9.2 %collective-permute-start.5 = (bf16[256,256]{1,0:T(8,128)(2,1)}, bf16[256,256]{1,0:T(8,128)(2,1)}, u32[]{:S(2)}, u32[]{:S(2)}) collective-permute-start(bf16[256,256]{1,0:T(8,128)(2,1)} %get-tuple-element.14), channel_id=1, source_target_pairs={{0,256},{8,264},{16,272},{24,280},{32,288},{40,296},{48,304},{56,3... | collective-permute-start | bytes 393224 | tf_op jit(solution)/shard_map/ppermute | solution.py:363
  97.0 0.0 all-to-all-done
  97.0 10.0 %prefill.1 = bf16[1024,1024]{1,0:T(8,128)(2,1)} custom-call(bf16[10240,128]{1,0:T(8,128)(2,1)S(1)} %bitcast.10, bf16[1024,128]{1,0:T(8,128)(2,1)S(1)} %get-tuple-element.9.mask_ref), custom_call_target="tpu_custom_call" | custom-call | tf_op jit(solution)/shard_map/prefill/pallas_call | solution.py:318
  107.0 0.0 collective-permute-done.1.refs_1_
  107.0 0.0 collective-permute-done.2.refs_2_
  107.0 0.0 collective-permute-done.3.refs_3_
  107.0 0.0 collective-permute-done.4.refs_4_
  107.0 0.0 collective-permute-done.5.refs_5_
  107.1 0.0 copy-done.7
  107.1 2.4 %traded.1 = bf16[32,1024]{1,0:T(8,128)(2,1)} custom-call(s32[1]{0:T(128)} %bitcast.inst_ref, s32[64]{0:T(128)S(1)} %copy-done.7, s32[64]{0:T(128)S(1)} %copy-done.6, s32[512]{0:T(512)S(1)} %copy-done.4, bf16[32,1024]{1,0:T(8,128)(2,1)S(1)} %bitcast.15, bf16[32,256]{1,0:T(8,128)(2,1)S(1)} %bitcast.17, bf16[32,1024]{1,0:T(8,128)(2,1)S(1)} %decode.1.decoded_ref, ...), custom_call_target="tpu_custom_call" | custom-call | tf_op jit(solution)/shard_map/traded/pallas_call | solution.py:241
Async XLA Ops:
  5.2 22.2 %copy-start.1 = (s32[32768,1]{0,1:T(1,128)S(1)}, s32[32768,1]{0,1:T(1,128)}, u32[]{:S(2)}) copy-start(s32[32768,1]{0,1:T(1,128)} %param.19) | copy-start | bytes 393220
  5.3 22.2 %copy-start.5 = (s32[8,16]{1,0:T(8,128)S(1)}, s32[8,16]{1,0:T(8,128)}, u32[]{:S(2)}) copy-start(s32[8,16]{1,0:T(8,128)} %table_ref.1) | copy-start | bytes 1540
  5.3 22.2 %copy-start.6 = (s32[64]{0:T(128)S(1)}, s32[64]{0:T(128)}, u32[]{:S(2)}) copy-start(s32[64]{0:T(128)} %slot_ref.3) | copy-start | bytes 772
  5.3 25.3 %copy-start.2 = (bf16[4,8,1024]{2,1,0:T(8,128)(2,1)S(1)}, bf16[4,8,1024]{2,1,0:T(8,128)(2,1)}, u32[]{:S(2)}) copy-start(bf16[4,8,1024]{2,1,0:T(8,128)(2,1)} %param.10) | copy-start | bytes 196612
  5.3 25.3 %copy-start.3 = (bf16[4,8,1,256]{3,1,2,0:T(8,128)(2,1)S(1)}, bf16[4,8,1,256]{3,1,2,0:T(8,128)(2,1)}, u32[]{:S(2)}) copy-start(bf16[4,8,1,256]{3,1,2,0:T(8,128)(2,1)} %param.11) | copy-start | bytes 49156
  5.3 25.2 %copy-start.4 = (s32[512]{0:T(512)S(1)}, s32[512]{0:T(512)}, u32[]{:S(2)}) copy-start(s32[512]{0:T(512)} %lens_ref.3) | copy-start | bytes 6148
  5.3 91.7 %all-to-all-start = ((bf16[512,5,4,128]{3,2,1,0:T(4,128)(2,1)}), bf16[512,5,4,128]{3,2,1,0:T(4,128)(2,1)S(1)}, u32[]{:S(2)}, u32[]{:S(2)}) async-start(bf16[512,5,4,128]{3,2,1,0:T(4,128)(2,1)} %bitcast.18), calls=%async_computation | async-start | bytes 5242880 | tf_op jit(solution)/shard_map/all_to_all | solution.py:352
  27.5 1.2 %copy-start = (bf16[128,16,1,256]{3,1,2,0:T(8,128)(2,1)S(1)}, bf16[128,16,1,256]{3,1,2,0:T(8,128)(2,1)}, u32[]{:S(2)}) copy-start(bf16[128,16,1,256]{3,1,2,0:T(8,128)(2,1)} %param.12) | copy-start | bytes 3145732
  32.1 74.9 %copy-start.7 = (s32[64]{0:T(128)S(1)}, s32[64]{0:T(128)}, u32[]{:S(2)}) copy-start(s32[64]{0:T(128)} %partner_ref.1) | copy-start | bytes 772
  32.2 55.6 %collective-permute-start = (bf16[256,256]{1,0:T(8,128)(2,1)}, bf16[256,256]{1,0:T(8,128)(2,1)S(1)}, u32[]{:S(2)}, u32[]{:S(2)}) collective-permute-start(bf16[256,256]{1,0:T(8,128)(2,1)} %get-tuple-element.14), channel_id=1, source_target_pairs={{0,8},{8,0},{16,24},{24,16},{32,40},{40,32},{48,56},{56,48},{64,72... | collective-permute-start | bytes 393224 | tf_op jit(solution)/shard_map/ppermute | solution.py:363
  35.5 71.6 %collective-permute-start.1 = (bf16[256,256]{1,0:T(8,128)(2,1)}, bf16[256,256]{1,0:T(8,128)(2,1)S(1)}, u32[]{:S(2)}, u32[]{:S(2)}) collective-permute-start(bf16[256,256]{1,0:T(8,128)(2,1)} %get-tuple-element.14), channel_id=1, source_target_pairs={{0,16},{8,24},{16,0},{24,8},{32,48},{40,56},{48,32},{56,40},{64,80... | collective-permute-start | bytes 393224 | tf_op jit(solution)/shard_map/ppermute | solution.py:363
  39.5 67.5 %collective-permute-start.2 = (bf16[256,256]{1,0:T(8,128)(2,1)}, bf16[256,256]{1,0:T(8,128)(2,1)S(1)}, u32[]{:S(2)}, u32[]{:S(2)}) collective-permute-start(bf16[256,256]{1,0:T(8,128)(2,1)} %get-tuple-element.14), channel_id=1, source_target_pairs={{0,32},{8,40},{16,48},{24,56},{32,0},{40,8},{48,16},{56,24},{64,96... | collective-permute-start | bytes 393224 | tf_op jit(solution)/shard_map/ppermute | solution.py:363
  44.1 62.9 %collective-permute-start.3 = (bf16[256,256]{1,0:T(8,128)(2,1)}, bf16[256,256]{1,0:T(8,128)(2,1)}, u32[]{:S(2)}, u32[]{:S(2)}) collective-permute-start(bf16[256,256]{1,0:T(8,128)(2,1)} %get-tuple-element.14), channel_id=1, source_target_pairs={{0,64},{8,72},{16,80},{24,88},{32,96},{40,104},{48,112},{56,120},{... | collective-permute-start | bytes 393224 | tf_op jit(solution)/shard_map/ppermute | solution.py:363
  47.2 59.8 %collective-permute-start.4 = (bf16[256,256]{1,0:T(8,128)(2,1)}, bf16[256,256]{1,0:T(8,128)(2,1)}, u32[]{:S(2)}, u32[]{:S(2)}) collective-permute-start(bf16[256,256]{1,0:T(8,128)(2,1)} %get-tuple-element.14), channel_id=1, source_target_pairs={{0,128},{8,136},{16,144},{24,152},{32,160},{40,168},{48,176},{56,1... | collective-permute-start | bytes 393224 | tf_op jit(solution)/shard_map/ppermute | solution.py:363
  87.7 19.3 %collective-permute-start.5 = (bf16[256,256]{1,0:T(8,128)(2,1)}, bf16[256,256]{1,0:T(8,128)(2,1)}, u32[]{:S(2)}, u32[]{:S(2)}) collective-permute-start(bf16[256,256]{1,0:T(8,128)(2,1)} %get-tuple-element.14), channel_id=1, source_target_pairs={{0,256},{8,264},{16,272},{24,280},{32,288},{40,296},{48,304},{56,3... | collective-permute-start | bytes 393224 | tf_op jit(solution)/shard_map/ppermute | solution.py:363

commit v4 on v3

--- a/solution.py
+++ b/solution.py
@@ -32,57 +32,62 @@
 NT = ((1,), (1,))
 
 
-INSTS = 32
-
-
-def dispatch_kernel(me_ref, target_ref, queries_ref, keyvals_ref, out_ref, place_ref, rows_ref):
-    step = pl.program_id(0)
-
-    @pl.when(step == 0)
-    def _():
-        me = me_ref[0]
-        line = lax.rem(lax.div(me, 2), 8)
-        both = jnp.sum(
-            jnp.where(iota((8, LANES), 0) == line, target_ref[...], 0), axis=0, keepdims=True
-        )
-        both = jnp.broadcast_to(both, (8, LANES))
-        other = pltpu.roll(both, ROWS_DEV, 1)
-        first = iota((8, LANES), 1) < ROWS_DEV
-        odd = lax.rem(me, 2) == 1
-        mine = jnp.where(first != odd, both, other)[0:1]
-        down, along = iota((ROWS_DEV, LANES), 0), iota((ROWS_DEV, LANES), 1)
-        wide = jnp.broadcast_to(mine, (ROWS_DEV, LANES))
-        column = jnp.sum(jnp.where(down == along, wide, 0), axis=1, keepdims=True)
-        earlier = (column == wide) & (down < along % ROWS_DEV)
-        rank = jnp.sum(earlier.astype(jnp.int32), axis=0, keepdims=True)
-        place = jnp.broadcast_to(mine * CAP + rank, (8, LANES))
-        for i in range(4):
-            place_ref[:, i * LANES : (i + 1) * LANES] = place
-        down, along = iota((512, 512), 0), iota((512, 512), 1)
-        order = (down % ROWS_DEV == along // KVH) & (down // ROWS_DEV == along % KVH)
-        keyvals = dot(order.astype(jnp.float32).astype(jnp.bfloat16), keyvals_ref[...])
-        keyvals = keyvals.astype(jnp.bfloat16)
-        for c in range(N_TP * TILES):
-            tp, tile = divmod(c, TILES)
-            if tile < GROUP:
-                piece = queries_ref[:, (tp * GROUP + tile) * HD : (tp * GROUP + tile + 1) * HD]
-            else:
-                lane = (tile - GROUP) * HD
-                piece = keyvals[tp * ROWS_DEV : (tp + 1) * ROWS_DEV, lane : lane + HD]
-            to, col = c % 8, c // 8
-            rows_ref[to * ROWS_DEV : (to + 1) * ROWS_DEV, col * LANES : (col + 1) * LANES] = piece
-
+INSTS = 16
+
+
+def dispatch_kernel(
+    me_ref, target_ref, queries_ref, keyvals_ref, out_hbm, rows_ref, out_ref, sems
+):
+    me = me_ref[0]
+    line = lax.rem(lax.div(me, 2), 8)
+    both = jnp.sum(
+        jnp.where(iota((8, LANES), 0) == line, target_ref[...], 0), axis=0, keepdims=True
+    )
+    both = jnp.broadcast_to(both, (8, LANES))
+    other = pltpu.roll(both, ROWS_DEV, 1)
+    first = iota((8, LANES), 1) < ROWS_DEV
+    odd = lax.rem(me, 2) == 1
+    mine = jnp.where(first != odd, both, other)[0:1]
+    down, along = iota((ROWS_DEV, LANES), 0), iota((ROWS_DEV, LANES), 1)
+    wide = jnp.broadcast_to(mine, (ROWS_DEV, LANES))
+    column = jnp.sum(jnp.where(down == along, wide, 0), axis=1, keepdims=True)
+    earlier = (column == wide) & (down < along % ROWS_DEV)
+    rank = jnp.sum(earlier.astype(jnp.int32), axis=0, keepdims=True)
+    place = jnp.concatenate([mine * CAP + rank] * 4, axis=1)
+    place = jnp.broadcast_to(place, (INSTS * 16, 512))
+    down, along = iota((512, 512), 0), iota((512, 512), 1)
+    order = (down % ROWS_DEV == along // KVH) & (down // ROWS_DEV == along % KVH)
+    keyvals = dot(order.astype(jnp.float32).astype(jnp.bfloat16), keyvals_ref[...])
+    keyvals = keyvals.astype(jnp.bfloat16)
+    for c in range(N_TP * TILES):
+        tp, tile = divmod(c, TILES)
+        if tile < GROUP:
+            piece = queries_ref[:, (tp * GROUP + tile) * HD : (tp * GROUP + tile + 1) * HD]
+        else:
+            lane = (tile - GROUP) * HD
+            piece = keyvals[tp * ROWS_DEV : (tp + 1) * ROWS_DEV, lane : lane + HD]
+        to, col = c % 8, c // 8
+        rows_ref[to * ROWS_DEV : (to + 1) * ROWS_DEV, col * LANES : (col + 1) * LANES] = piece
     down, along = iota((INSTS * 16, 512), 0), iota((INSTS * 16, 512), 1)
-    wanted = (step * INSTS + down // 16) * CAP + down % 2
-    place = jnp.broadcast_to(place_ref[0:1, :], (INSTS * 16, 512))
-    chosen = (place == wanted) & (along // ROWS_DEV == down // 2 % 8)
-    out = dot(chosen.astype(jnp.float32).astype(jnp.bfloat16), rows_ref[...])
-    out = out.astype(jnp.bfloat16)
-    for i in range(INSTS):
-        for col in range(TILES):
-            out_ref[i * 160 + col * 16 : i * 160 + (col + 1) * 16, :] = out[
-                i * 16 : (i + 1) * 16, col * LANES : (col + 1) * LANES
-            ]
+    here = along // ROWS_DEV == down // 2 % 8
+    wanted = down // 16 * CAP + down % 2
+    size = INSTS * N_TP * MESSAGE
+    copies = []
+    for step in range(N_INST // INSTS):
+        chosen = (place == wanted + step * INSTS * CAP) & here
+        out = dot(chosen.astype(jnp.float32).astype(jnp.bfloat16), rows_ref[...])
+        out = out.astype(jnp.bfloat16)
+        for i in range(INSTS):
+            for col in range(TILES):
+                row = step * size + i * 160 + col * 16
+                out_ref[row : row + 16, :] = out[
+                    i * 16 : (i + 1) * 16, col * LANES : (col + 1) * LANES
+                ]
+        rows = pl.ds(step * size, size)
+        copies.append(pltpu.make_async_copy(out_ref.at[rows], out_hbm.at[rows], sems.at[step]))
+        copies[-1].start()
+    for copy in copies:
+        copy.wait()
 
 
 def dispatch(me, targets, queries, keyvals):
@@ -92,16 +97,17 @@
         out_shape=pltpu.HBM((rows, LANES), jnp.bfloat16),
         grid_spec=pltpu.PrefetchScalarGridSpec(
             num_scalar_prefetch=1,
-            grid=(N_INST // INSTS,),
+            grid=(1,),
             in_specs=[
                 pl.BlockSpec((8, LANES), lambda s, me: (me[0] // 16, 0)),
                 pl.BlockSpec((ROWS_DEV, H * HD), lambda s, me: (0, 0)),
                 pl.BlockSpec((ROWS_DEV * KVH, 2 * HD), lambda s, me: (0, 0)),
             ],
-            out_specs=pl.BlockSpec((rows * INSTS // N_INST, LANES), lambda s, me: (s, 0)),
+            out_specs=pl.BlockSpec(memory_space=pltpu.HBM),
             scratch_shapes=[
-                pltpu.VMEM((8, 512), jnp.int32),
                 pltpu.VMEM((512, TILES * LANES), jnp.bfloat16),
+                pltpu.VMEM((rows, LANES), jnp.bfloat16),
+                pltpu.SemaphoreType.DMA((N_INST // INSTS,)),
             ],
         ),
         compiler_params=pltpu.CompilerParams(vmem_limit_bytes=VMEM),
@@ -151,7 +157,10 @@
     )(inst, slots, table, cache, targets)
 
 
-def decode_kernel(inst_ref, lens_ref, queries_ref, fresh_ref, context_ref, out_ref):
+def decode_kernel(
+    inst_ref, slot_ref, lens_ref, queries_ref, fresh_ref, context_ref,
+    out_ref, query_ref, newer_ref, values_ref,
+):
     inst = inst_ref[0]
     rows = STEPS * REQ
     queries, fresh = queries_ref[...], fresh_ref[...]
@@ -177,6 +186,21 @@
     for g in range(GROUP):
         out_ref[:, g * HD : (g + 1) * HD] = out[g * rows : (g + 1) * rows].astype(jnp.bfloat16)
 
+    moved = slot_ref[inst]
+    chosen = iota((8, rows), 1) == iota((8, rows), 0) * REQ + moved
+    picked = dot(chosen.astype(jnp.float32).astype(jnp.bfloat16), queries)
+    picked = jnp.concatenate([picked[:, g * HD : (g + 1) * HD] for g in range(GROUP)], axis=0)
+    picked = picked.astype(jnp.bfloat16)
+    query_ref[...] = picked
+    chosen = iota((LANES, rows), 1) == iota((LANES, rows), 0) * REQ + moved
+    fresh = dot(chosen.astype(jnp.float32).astype(jnp.bfloat16), fresh).astype(jnp.bfloat16)
+    values_ref[...] = fresh[:, HD:]
+    shape = newer_ref.shape
+    moment, along = iota(shape, 0) % 8, iota(shape, 1)
+    newer_ref[...] = jnp.where(
+        (along <= moment) & (along < STEPS), dot(picked, fresh[:, :HD], NT), MASKED
+    )
+
 
 def shares(past, newer):
     top = jnp.maximum(
@@ -188,23 +212,28 @@
     return past / total, newer / total
 
 
-def decode(inst, lens, queries, fresh, context):
+def decode(inst, slots, lens, queries, fresh, context):
     smem, vmem = pltpu.SMEM, pltpu.VMEM
     return pl.pallas_call(
         decode_kernel,
-        out_shape=jax.ShapeDtypeStruct(queries.shape, jnp.bfloat16),
-        in_specs=specs(smem, smem, vmem, vmem, vmem),
-        out_specs=specs(vmem)[0],
+        out_shape=(
+            jax.ShapeDtypeStruct(queries.shape, jnp.bfloat16),
+            jax.ShapeDtypeStruct((GROUP * 8, HD), jnp.bfloat16),
+            jax.ShapeDtypeStruct((GROUP * 8, LANES), jnp.float32),
+            jax.ShapeDtypeStruct((LANES, HD), jnp.bfloat16),
+        ),
+        in_specs=specs(smem, smem, smem, vmem, vmem, vmem),
+        out_specs=specs(vmem, vmem, vmem, vmem),
         compiler_params=pltpu.CompilerParams(vmem_limit_bytes=VMEM),
         name="decode",
-    )(inst, lens, queries, fresh, context)
+    )(inst, slots, lens, queries, fresh, context)
 
 
 BITS = N_INST.bit_length() - 1
 
 
 def traded_kernel(
-    inst_ref, partner_ref, slot_ref, lens_ref, queries_ref, fresh_ref, decoded_ref, *refs
+    inst_ref, partner_ref, slot_ref, lens_ref, query_ref, newer_ref, values_ref, decoded_ref, *refs
 ):
     *came_refs, out_ref = refs
     inst = inst_ref[0]
@@ -214,45 +243,38 @@
     came = came_refs[0][...]
     for bit in range(1, BITS):
         came = jnp.where(distance == 1 << bit, came_refs[bit][...], came)
-    rows = STEPS * REQ
-    chosen = iota((8, rows), 1) == iota((8, rows), 0) * REQ + moved
-    chosen = chosen.astype(jnp.float32).astype(jnp.bfloat16)
-    queries = dot(chosen, queries_ref[...])
-    fresh = dot(chosen, fresh_ref[...]).astype(jnp.bfloat16)
-    query = jnp.concatenate([queries[:, g * HD : (g + 1) * HD] for g in range(GROUP)], axis=0)
-    query = query.astype(jnp.bfloat16)
-    n = GROUP * 8
-    newer = dot(query, fresh[:, :HD], NT)
-    moment, along = iota((n, 8), 0) % 8, iota((n, 8), 1)
-    newer = jnp.where((along <= moment) & (along < STEPS), newer, MASKED)
+    past = dot(query_ref[...], came[:, :HD], NT)
     length = lens_ref[other * REQ + slot_ref[other]]
-    past = jnp.where(iota((n, CTX), 1) < length, dot(query, came[:, :HD], NT), MASKED)
-    past, newer = shares(past, newer)
+    past = jnp.where(iota(past.shape, 1) < length, past, MASKED)
+    past, newer = shares(past, newer_ref[...])
     out = dot(past.astype(jnp.bfloat16), came[:, HD:])
-    out = out + dot(newer.astype(jnp.bfloat16), fresh[:, HD:])
+    out = out + dot(newer.astype(jnp.bfloat16), values_ref[...])
     out = jnp.concatenate([out[g * 8 : (g + 1) * 8] for g in range(GROUP)], axis=1)
-    out = dot(chosen, out.astype(jnp.bfloat16), ((0,), (0,)))
+    rows, width = out_ref.shape
+    out = jnp.broadcast_to(out[:STEPS, None, :], (STEPS, REQ, width)).reshape(rows, width)
     here = iota((rows, 1), 0) % REQ == moved
     out_ref[...] = jnp.where(here, out, decoded_ref[...].astype(jnp.float32)).astype(jnp.bfloat16)
 
 
-def traded(inst, partner, slots, lens, queries, fresh, decoded, came):
+def traded(inst, partner, slots, lens, query, newer, values, decoded, came):
     smem, vmem = pltpu.SMEM, pltpu.VMEM
     return pl.pallas_call(
         traded_kernel,
-        out_shape=jax.ShapeDtypeStruct(queries.shape, jnp.bfloat16),
-        in_specs=specs(*[smem] * 4, *[vmem] * (3 + BITS)),
+        out_shape=jax.ShapeDtypeStruct(decoded.shape, jnp.bfloat16),
+        in_specs=specs(*[smem] * 4, *[vmem] * (4 + BITS)),
         out_specs=specs(vmem)[0],
         compiler_params=pltpu.CompilerParams(vmem_limit_bytes=VMEM),
         name="traded",
-    )(inst, partner, slots, lens, queries, fresh, decoded, *came)
+    )(inst, partner, slots, lens, query, newer, values, decoded, *came)
 
 
 BLOCK = 128
 HEADS = 4
 
 
-def prefill_kernel(arrived_ref, mask_ref, out_ref, packed_ref, keys_ref, last_ref, values_ref):
+def prefill_kernel(
+    arrived_ref, mask_ref, out_hbm, packed_ref, keys_ref, last_ref, values_ref, out_ref, sems
+):
     size = N_TP * MESSAGE
     to, src = iota((size, size), 0), iota((size, size), 1)
     order = (
@@ -300,6 +322,7 @@
         for h in range(0, GROUP, HEADS)
     ]
     scores = scored(*work[0])
+    copies = []
     for i, (start, end, heads) in enumerate(work):
         ahead = scored(*work[i + 1]) if i + 1 < len(work) else None
         filled = (mask_ref[start:end, 0:1].astype(jnp.float32) == 0).astype(jnp.float32)
@@ -310,7 +333,13 @@
         out = (out[:, :HD] * (filled / out[:, HD:])).astype(jnp.bfloat16)
         for j, h in enumerate(heads):
             out_ref[start:end, h * HD : (h + 1) * HD] = out[j * BLOCK : (j + 1) * BLOCK]
+        if heads[-1] == GROUP - 1:
+            rows, sem = pl.ds(start, BLOCK), sems.at[start // BLOCK]
+            copies.append(pltpu.make_async_copy(out_ref.at[rows], out_hbm.at[rows], sem))
+            copies[-1].start()
         scores = ahead
+    for copy in copies:
+        copy.wait()
 
 
 def prefill(arrived, mask):
@@ -319,12 +348,14 @@
         prefill_kernel,
         out_shape=jax.ShapeDtypeStruct((SLOTS, GROUP * HD), jnp.bfloat16),
         in_specs=specs(vmem, vmem),
-        out_specs=specs(vmem)[0],
+        out_specs=specs(pltpu.HBM)[0],
         scratch_shapes=[
             pltpu.VMEM((TILES, SLOTS, LANES), jnp.bfloat16),
             pltpu.VMEM((SLOTS, 2 * HD), jnp.bfloat16),
             pltpu.VMEM((SLOTS, 2 * HD), jnp.bfloat16),
             pltpu.VMEM((SLOTS, 2 * HD), jnp.bfloat16),
+            pltpu.VMEM((SLOTS, GROUP * HD), jnp.bfloat16),
+            pltpu.SemaphoreType.DMA((SLOTS // BLOCK,)),
         ],
         compiler_params=pltpu.CompilerParams(vmem_limit_bytes=VMEM),
         name="prefill",
@@ -357,15 +388,19 @@
     leaving, context, mask = prepare(inst[None], moved_slot, block_table, cache, targets)
     queries = step_queries.reshape(STEPS * REQ, GROUP * HD)
     fresh = step_keyvals.reshape(STEPS * REQ, 2 * HD)
-    decoded = decode(inst[None], context_len, queries, fresh, context)
+    decoded, query, newer, values = decode(
+        inst[None], moved_slot, context_len, queries, fresh, context
+    )
     leaving, decoded = lax.optimization_barrier((leaving, decoded))
     came = [
         lax.ppermute(leaving, "inst", [(i, i ^ 1 << bit) for i in range(N_INST)])
         for bit in range(BITS)
     ]
     prefill_output = prefill(arrived, mask)
-    queries, prefill_output = lax.optimization_barrier((queries, prefill_output))
-    decoded = traded(inst[None], partner, moved_slot, context_len, queries, fresh, decoded, came)
+    query, prefill_output = lax.optimization_barrier((query, prefill_output))
+    decoded = traded(
+        inst[None], partner, moved_slot, context_len, query, newer, values, decoded, came
+    )
     return decoded.reshape(step_queries.shape), prefill_output
 
 

time: 111 us -> 110 us (level)
  waiting for transfers between devices: 36.2 us -> 34.3 us
  local copies, waits for them, and re-layouts: 1.25 us -> 3.12 us
  Pallas kernels: 20.4 us -> 19.2 us
    ppermute x6, waiting for transfers between devices: 36.2 us -> 34.3 us  [local(): lax.ppermute(leaving, 'inst', [(i, i ^ 1 << bit) for i in range(N_INST)])]
    unnamed x16 -> x32, local copies, waits for them, and re-layouts: 1.25 us -> 3.12 us
where the time goes in v4:
time: 110 us; the launch traced here: 108 us
  starting transfers between devices  50.7 us (46%)
  waiting for transfers between devices  34.3 us (31%)
  Pallas kernels  19.2 us (17%)
  local copies, waits for them, and re-layouts  3.12 us (3%)
    ppermute x6, waiting for transfers between devices, local(): lax.ppermute(leaving, 'inst', [(i, i ^ 1 << bit) for i in range(N_INST)])  34.3 us
    ppermute x6, starting transfers between devices, local(): lax.ppermute(leaving, 'inst', [(i, i ^ 1 << bit) for i in range(N_INST)])  28.6 us
    all_to_all x1, starting transfers between devices, local(): lax.all_to_all(sent.reshape(N_INST * N_TP, MESSAGE // 4, 4, LANES), ('ins...  22.2 us
    pallas_call x1, Pallas kernels, prefill(): pl.pallas_call(prefill_kernel, out_shape=jax.ShapeDtypeStruct((SLOTS, GRO...  9.44 us
    pallas_call x1, Pallas kernels, dispatch(): pl.pallas_call(dispatch_kernel, out_shape=pltpu.HBM((rows, LANES), jnp.bf...  4.18 us
    unnamed x32, local copies, waits for them, and re-layouts  3.12 us
  transfers between devices with their start and end apart: 7, of which 1 were waited for; matrix products, arithmetic and copies ran while one was open for 0% of the time, Pallas kernels for 12%

profile of v4, /device:TPU:1, one launch (start us, length us, event | category | flops | bytes accessed | tf_op | source)
XLA Modules:
  0.0 108.3 jit_solution(9942734261504399557)
XLA Ops:
  0.6 4.2 %dispatch.1 = bf16[10240,128]{1,0:T(8,128)(2,1)} custom-call(s32[1]{0:T(128)} %bitcast.5.me_ref, s32[256,128]{1,0:T(8,128)} %bitcast.12, bf16[64,8192]{1,0:T(8,128)(2,1)} %queries_ref.1, bf16[512,256]{1,0:T(8,128)(2,1)} %bitcast.17), custom_call_target="tpu_custom_call" | custom-call | tf_op jit(solution)/shard_map/dispatch/pallas_call | solution.py:95
  4.8 0.0 copy-start.1
  4.8 0.0 copy-start.12
  4.8 0.0 copy-start.14
  4.9 0.0 copy-start.2
  4.9 0.0 copy-start.9
  4.9 0.0 copy-start.10
  4.9 22.2 %all-to-all-start = ((bf16[512,5,4,128]{3,2,1,0:T(4,128)(2,1)}), bf16[512,5,4,128]{3,2,1,0:T(4,128)(2,1)S(1)}, u32[]{:S(2)}, u32[]{:S(2)}) async-start(bf16[512,5,4,128]{3,2,1,0:T(4,128)(2,1)} %bitcast.16), calls=%async_computation | async-start | bytes 5242880 | tf_op jit(solution)/shard_map/all_to_all | solution.py:383
  27.1 0.0 copy-done.1
  27.1 0.0 copy-done.12
  27.1 0.0 copy-done.14
  27.1 0.0 copy-start
  27.1 1.2 %copy-done = bf16[128,16,1,256]{3,1,2,0:T(8,128)(2,1)S(1)} copy-done((bf16[128,16,1,256]{3,1,2,0:T(8,128)(2,1)S(1)}, bf16[128,16,1,256]{3,1,2,0:T(8,128)(2,1)}, u32[]{:S(2)}) %copy-start) | copy-done | bytes 1048600
  28.3 1.8 %prepare.1 = (bf16[256,256]{1,0:T(8,128)(2,1)}, bf16[2048,256]{1,0:T(8,128)(2,1)S(1)}, bf16[1024,128]{1,0:T(8,128)(2,1)S(1)}) custom-call(s32[1]{0:T(128)} %bitcast.inst_ref, s32[64]{0:T(128)S(1)} %copy-done.12, s32[8,16]{1,0:T(8,128)S(1)} %copy-done.14, bf16[2048,256]{1,0:T(8,128)(2,1)S(1)} %bitcast.11, s32[256,128]{1,0:T(8,128)S(1)} %bitcast.13), custom_call_target="tpu_custom_call" | custom-call | tf_op jit(solution)/shard_map/prepare/pallas_call | solution.py:146
  30.1 0.0 copy-done.2
  30.1 0.0 copy-done.9
  30.1 0.0 copy-done.10
  30.1 1.7 %decode.1 = (bf16[32,1024]{1,0:T(8,128)(2,1)S(1)}, bf16[64,128]{1,0:T(8,128)(2,1)S(1)}, f32[64,128]{1,0:T(8,128)S(1)}, bf16[128,128]{1,0:T(8,128)(2,1)S(1)}) custom-call(s32[1]{0:T(128)} %bitcast.inst_ref, s32[64]{0:T(128)S(1)} %copy-done.12, s32[512]{0:T(512)S(1)} %copy-done.10, bf16[32,1024]{1,0:T(8,128)(2,1)S(1)} %bitcast.14, ...), custom_call_target="tpu_custom_call" | custom-call | tf_op jit(solution)/shard_map/decode/pallas_call | solution.py:217
  31.9 0.6 copy-done.3
  32.5 0.6 copy-done.5
  33.1 0.6 copy-done.7
  33.7 3.3 %collective-permute-start = (bf16[256,256]{1,0:T(8,128)(2,1)}, bf16[256,256]{1,0:T(8,128)(2,1)S(1)}, u32[]{:S(2)}, u32[]{:S(2)}) collective-permute-start(bf16[256,256]{1,0:T(8,128)(2,1)} %get-tuple-element.22), channel_id=1, source_target_pairs={{0,8},{8,0},{16,24},{24,16},{32,40},{40,32},{48,56},{56,48},{64,72... | collective-permute-start | bytes 393224 | tf_op jit(solution)/shard_map/ppermute | solution.py:396
  37.0 4.0 %collective-permute-start.1 = (bf16[256,256]{1,0:T(8,128)(2,1)}, bf16[256,256]{1,0:T(8,128)(2,1)S(1)}, u32[]{:S(2)}, u32[]{:S(2)}) collective-permute-start(bf16[256,256]{1,0:T(8,128)(2,1)} %get-tuple-element.22), channel_id=1, source_target_pairs={{0,16},{8,24},{16,0},{24,8},{32,48},{40,56},{48,32},{56,40},{64,80... | collective-permute-start | bytes 393224 | tf_op jit(solution)/shard_map/ppermute | solution.py:396
  41.0 4.6 %collective-permute-start.2 = (bf16[256,256]{1,0:T(8,128)(2,1)}, bf16[256,256]{1,0:T(8,128)(2,1)S(1)}, u32[]{:S(2)}, u32[]{:S(2)}) collective-permute-start(bf16[256,256]{1,0:T(8,128)(2,1)} %get-tuple-element.22), channel_id=1, source_target_pairs={{0,32},{8,40},{16,48},{24,56},{32,0},{40,8},{48,16},{56,24},{64,96... | collective-permute-start | bytes 393224 | tf_op jit(solution)/shard_map/ppermute | solution.py:396
  45.6 3.1 %collective-permute-start.3 = (bf16[256,256]{1,0:T(8,128)(2,1)}, bf16[256,256]{1,0:T(8,128)(2,1)S(1)}, u32[]{:S(2)}, u32[]{:S(2)}) collective-permute-start(bf16[256,256]{1,0:T(8,128)(2,1)} %get-tuple-element.22), channel_id=1, source_target_pairs={{0,64},{8,72},{16,80},{24,88},{32,96},{40,104},{48,112},{56,120},{... | collective-permute-start | bytes 393224 | tf_op jit(solution)/shard_map/ppermute | solution.py:396
  48.7 4.3 %collective-permute-start.4 = (bf16[256,256]{1,0:T(8,128)(2,1)}, bf16[256,256]{1,0:T(8,128)(2,1)S(1)}, u32[]{:S(2)}, u32[]{:S(2)}) collective-permute-start(bf16[256,256]{1,0:T(8,128)(2,1)} %get-tuple-element.22), channel_id=1, source_target_pairs={{0,128},{8,136},{16,144},{24,152},{32,160},{40,168},{48,176},{56,1... | collective-permute-start | bytes 393224 | tf_op jit(solution)/shard_map/ppermute | solution.py:396
  53.1 34.3 %collective-permute-done.refs_0_ = bf16[256,256]{1,0:T(8,128)(2,1)S(1)} collective-permute-done((bf16[256,256]{1,0:T(8,128)(2,1)}, bf16[256,256]{1,0:T(8,128)(2,1)S(1)}, u32[]{:S(2)}, u32[]{:S(2)}) %collective-permute-start) | collective-permute-done | bytes 131104 | tf_op jit(solution)/shard_map/ppermute | solution.py:396
  87.3 9.2 %collective-permute-start.5 = (bf16[256,256]{1,0:T(8,128)(2,1)}, bf16[256,256]{1,0:T(8,128)(2,1)}, u32[]{:S(2)}, u32[]{:S(2)}) collective-permute-start(bf16[256,256]{1,0:T(8,128)(2,1)} %get-tuple-element.22), channel_id=1, source_target_pairs={{0,256},{8,264},{16,272},{24,280},{32,288},{40,296},{48,304},{56,3... | collective-permute-start | bytes 393224 | tf_op jit(solution)/shard_map/ppermute | solution.py:396
  96.6 0.0 all-to-all-done
  96.6 0.0 copy-start.4
  96.6 0.0 copy-start.6
  96.6 0.0 copy-start.8
  96.6 0.0 copy-start.11
  96.6 0.0 copy-start.13
  96.6 0.0 copy-start.15
  96.7 9.4 %prefill.1 = bf16[1024,1024]{1,0:T(8,128)(2,1)} custom-call(bf16[10240,128]{1,0:T(8,128)(2,1)S(1)} %bitcast.10, bf16[1024,128]{1,0:T(8,128)(2,1)S(1)} %get-tuple-element.15.mask_ref), custom_call_target="tpu_custom_call" | custom-call | tf_op jit(solution)/shard_map/prefill/pallas_call | solution.py:347
  106.1 0.0 collective-permute-done.1.refs_1_
  106.1 0.0 collective-permute-done.2.refs_2_
  106.1 0.0 collective-permute-done.3.refs_3_
  106.1 0.0 collective-permute-done.4.refs_4_
  106.1 0.0 collective-permute-done.5.refs_5_
  106.2 0.0 copy-done.4
  106.2 0.0 copy-done.6
  106.2 0.0 copy-done.8
  106.2 0.0 copy-done.11
  106.2 0.0 copy-done.13
  106.2 0.0 copy-done.15
  106.2 2.1 %traded.1 = bf16[32,1024]{1,0:T(8,128)(2,1)} custom-call(s32[1]{0:T(128)} %bitcast.inst_ref, s32[64]{0:T(128)S(1)} %copy-done.15, s32[64]{0:T(128)S(1)} %copy-done.13, s32[512]{0:T(512)S(1)} %copy-done.11, bf16[64,128]{1,0:T(8,128)(2,1)S(1)} %get-tuple-element.16.query_ref, f32[64,128]{1,0:T(8,128)S(1)} %copy-done.6, bf16[128,128]{1,0:T(8,128)(2,1)S(1)} %copy-done.8, ...), custom_call_target="tpu_custom_call" | custom-call | tf_op jit(solution)/shard_map/traded/pallas_call | solution.py:261
  (3 shorter events, 0.0 us)
Async XLA Ops:
  4.8 22.2 %copy-start.1 = (s32[32768,1]{0,1:T(1,128)S(1)}, s32[32768,1]{0,1:T(1,128)}, u32[]{:S(2)}) copy-start(s32[32768,1]{0,1:T(1,128)} %param.19) | copy-start | bytes 393220
  4.8 22.2 %copy-start.12 = (s32[64]{0:T(128)S(1)}, s32[64]{0:T(128)}, u32[]{:S(2)}) copy-start(s32[64]{0:T(128)} %slot_ref.5) | copy-start | bytes 772
  4.8 22.2 %copy-start.14 = (s32[8,16]{1,0:T(8,128)S(1)}, s32[8,16]{1,0:T(8,128)}, u32[]{:S(2)}) copy-start(s32[8,16]{1,0:T(8,128)} %table_ref.1) | copy-start | bytes 1540
  4.9 25.3 %copy-start.2 = (bf16[4,8,1024]{2,1,0:T(8,128)(2,1)S(1)}, bf16[4,8,1024]{2,1,0:T(8,128)(2,1)}, u32[]{:S(2)}) copy-start(bf16[4,8,1024]{2,1,0:T(8,128)(2,1)} %param.10) | copy-start | bytes 196612
  4.9 25.3 %copy-start.9 = (bf16[4,8,1,256]{3,1,2,0:T(8,128)(2,1)S(1)}, bf16[4,8,1,256]{3,1,2,0:T(8,128)(2,1)}, u32[]{:S(2)}) copy-start(bf16[4,8,1,256]{3,1,2,0:T(8,128)(2,1)} %param.11) | copy-start | bytes 49156
  4.9 25.2 %copy-start.10 = (s32[512]{0:T(512)S(1)}, s32[512]{0:T(512)}, u32[]{:S(2)}) copy-start(s32[512]{0:T(512)} %lens_ref.3) | copy-start | bytes 6148
  4.9 91.7 %all-to-all-start = ((bf16[512,5,4,128]{3,2,1,0:T(4,128)(2,1)}), bf16[512,5,4,128]{3,2,1,0:T(4,128)(2,1)S(1)}, u32[]{:S(2)}, u32[]{:S(2)}) async-start(bf16[512,5,4,128]{3,2,1,0:T(4,128)(2,1)} %bitcast.16), calls=%async_computation | async-start | bytes 5242880 | tf_op jit(solution)/shard_map/all_to_all | solution.py:383
  27.1 1.2 %copy-start = (bf16[128,16,1,256]{3,1,2,0:T(8,128)(2,1)S(1)}, bf16[128,16,1,256]{3,1,2,0:T(8,128)(2,1)}, u32[]{:S(2)}) copy-start(bf16[128,16,1,256]{3,1,2,0:T(8,128)(2,1)} %param.12) | copy-start | bytes 3145732
  31.9 0.6 copy-start.3
  32.5 0.6 copy-start.5
  33.1 0.6 copy-start.7
  33.7 53.6 %collective-permute-start = (bf16[256,256]{1,0:T(8,128)(2,1)}, bf16[256,256]{1,0:T(8,128)(2,1)S(1)}, u32[]{:S(2)}, u32[]{:S(2)}) collective-permute-start(bf16[256,256]{1,0:T(8,128)(2,1)} %get-tuple-element.22), channel_id=1, source_target_pairs={{0,8},{8,0},{16,24},{24,16},{32,40},{40,32},{48,56},{56,48},{64,72... | collective-permute-start | bytes 393224 | tf_op jit(solution)/shard_map/ppermute | solution.py:396
  37.0 69.1 %collective-permute-start.1 = (bf16[256,256]{1,0:T(8,128)(2,1)}, bf16[256,256]{1,0:T(8,128)(2,1)S(1)}, u32[]{:S(2)}, u32[]{:S(2)}) collective-permute-start(bf16[256,256]{1,0:T(8,128)(2,1)} %get-tuple-element.22), channel_id=1, source_target_pairs={{0,16},{8,24},{16,0},{24,8},{32,48},{40,56},{48,32},{56,40},{64,80... | collective-permute-start | bytes 393224 | tf_op jit(solution)/shard_map/ppermute | solution.py:396
  41.0 65.1 %collective-permute-start.2 = (bf16[256,256]{1,0:T(8,128)(2,1)}, bf16[256,256]{1,0:T(8,128)(2,1)S(1)}, u32[]{:S(2)}, u32[]{:S(2)}) collective-permute-start(bf16[256,256]{1,0:T(8,128)(2,1)} %get-tuple-element.22), channel_id=1, source_target_pairs={{0,32},{8,40},{16,48},{24,56},{32,0},{40,8},{48,16},{56,24},{64,96... | collective-permute-start | bytes 393224 | tf_op jit(solution)/shard_map/ppermute | solution.py:396
  45.6 60.5 %collective-permute-start.3 = (bf16[256,256]{1,0:T(8,128)(2,1)}, bf16[256,256]{1,0:T(8,128)(2,1)S(1)}, u32[]{:S(2)}, u32[]{:S(2)}) collective-permute-start(bf16[256,256]{1,0:T(8,128)(2,1)} %get-tuple-element.22), channel_id=1, source_target_pairs={{0,64},{8,72},{16,80},{24,88},{32,96},{40,104},{48,112},{56,120},{... | collective-permute-start | bytes 393224 | tf_op jit(solution)/shard_map/ppermute | solution.py:396
  48.7 57.4 %collective-permute-start.4 = (bf16[256,256]{1,0:T(8,128)(2,1)}, bf16[256,256]{1,0:T(8,128)(2,1)S(1)}, u32[]{:S(2)}, u32[]{:S(2)}) collective-permute-start(bf16[256,256]{1,0:T(8,128)(2,1)} %get-tuple-element.22), channel_id=1, source_target_pairs={{0,128},{8,136},{16,144},{24,152},{32,160},{40,168},{48,176},{56,1... | collective-permute-start | bytes 393224 | tf_op jit(solution)/shard_map/ppermute | solution.py:396
  87.3 18.8 %collective-permute-start.5 = (bf16[256,256]{1,0:T(8,128)(2,1)}, bf16[256,256]{1,0:T(8,128)(2,1)}, u32[]{:S(2)}, u32[]{:S(2)}) collective-permute-start(bf16[256,256]{1,0:T(8,128)(2,1)} %get-tuple-element.22), channel_id=1, source_target_pairs={{0,256},{8,264},{16,272},{24,280},{32,288},{40,296},{48,304},{56,3... | collective-permute-start | bytes 393224 | tf_op jit(solution)/shard_map/ppermute | solution.py:396
  96.6 9.6 %copy-start.4 = (bf16[32,1024]{1,0:T(8,128)(2,1)S(1)}, bf16[32,1024]{1,0:T(8,128)(2,1)}, u32[]{:S(2)}) copy-start(bf16[32,1024]{1,0:T(8,128)(2,1)} %copy-done.3) | copy-start | bytes 196612
  96.6 9.6 %copy-start.6 = (f32[64,128]{1,0:T(8,128)S(1)}, f32[64,128]{1,0:T(8,128)}, u32[]{:S(2)}) copy-start(f32[64,128]{1,0:T(8,128)} %copy-done.5) | copy-start | bytes 98308
  96.6 9.6 %copy-start.8 = (bf16[128,128]{1,0:T(8,128)(2,1)S(1)}, bf16[128,128]{1,0:T(8,128)(2,1)}, u32[]{:S(2)}) copy-start(bf16[128,128]{1,0:T(8,128)(2,1)} %copy-done.7) | copy-start | bytes 98308
  96.6 9.6 %copy-start.11 = (s32[512]{0:T(512)S(1)}, s32[512]{0:T(512)}, u32[]{:S(2)}) copy-start(s32[512]{0:T(512)} %lens_ref.3) | copy-start | bytes 6148
  96.6 9.6 %copy-start.13 = (s32[64]{0:T(128)S(1)}, s32[64]{0:T(128)}, u32[]{:S(2)}) copy-start(s32[64]{0:T(128)} %slot_ref.5) | copy-start | bytes 772
  96.6 9.6 %copy-start.15 = (s32[64]{0:T(128)S(1)}, s32[64]{0:T(128)}, u32[]{:S(2)}) copy-start(s32[64]{0:T(128)} %partner_ref.1) | copy-start | bytes 772

commit v5 on v4

--- a/solution.py
+++ b/solution.py
@@ -269,11 +269,11 @@
 
 
 BLOCK = 128
-HEADS = 4
+HEADS = 8
 
 
 def prefill_kernel(
-    arrived_ref, mask_ref, out_hbm, packed_ref, keys_ref, last_ref, values_ref, out_ref, sems
+    arrived_ref, mask_ref, out_hbm, packed_ref, keys_ref, values_ref, out_ref, sems
 ):
     size = N_TP * MESSAGE
     to, src = iota((size, size), 0), iota((size, size), 1)
@@ -297,12 +297,11 @@
                 packed_ref[tile, start + j * 16 : start + (j + 1) * 16, :] = rows[
                     tile * 16 : (tile + 1) * 16, j * LANES : (j + 1) * LANES
                 ]
-        mask = mask_ref[start:end, :]
         keys_ref[start:end, :HD] = packed_ref[GROUP, start:end, :]
-        keys_ref[start:end, HD:] = mask
-        last_ref[start:end, :HD] = packed_ref[GROUP, start:end, :]
-        mask = jnp.where(late, MASKED, mask.astype(jnp.float32))
-        last_ref[start:end, HD:] = mask.astype(jnp.bfloat16)
+        mask = jnp.where(late, MASKED, mask_ref[start:end, :].astype(jnp.float32))
+        keys_ref[start:end, HD:] = mask.astype(jnp.bfloat16)
+        if start:
+            keys_ref[start - BLOCK : start, HD:] = mask_ref[start - BLOCK : start, :]
         values_ref[start:end, :HD] = packed_ref[GROUP + 1, start:end, :]
         values_ref[start:end, HD:] = jnp.ones((BLOCK, LANES), jnp.bfloat16)
 
@@ -311,10 +310,7 @@
             bring(start, end)
         query = jnp.concatenate([packed_ref[h, start:end, :] for h in heads], axis=0)
         query = jnp.concatenate([query, positions], axis=1)
-        scores = dot(query, last_ref[start:end, :], NT)
-        if start:
-            scores = jnp.concatenate([dot(query, keys_ref[:start, :], NT), scores], axis=1)
-        return scores
+        return dot(query, keys_ref[:end, :], NT)
 
     work = [
         (start, start + BLOCK, range(h, h + HEADS))
@@ -353,7 +349,6 @@
             pltpu.VMEM((TILES, SLOTS, LANES), jnp.bfloat16),
             pltpu.VMEM((SLOTS, 2 * HD), jnp.bfloat16),
             pltpu.VMEM((SLOTS, 2 * HD), jnp.bfloat16),
-            pltpu.VMEM((SLOTS, 2 * HD), jnp.bfloat16),
             pltpu.VMEM((SLOTS, GROUP * HD), jnp.bfloat16),
             pltpu.SemaphoreType.DMA((SLOTS // BLOCK,)),
         ],

time: 110 us -> 110 us (level)
  no operation moved by 1% of the time
where the time goes in v5:
time: 110 us; the launch traced here: 108 us
  starting transfers between devices  50.7 us (46%)
  waiting for transfers between devices  34.3 us (31%)
  Pallas kernels  18.7 us (17%)
  local copies, waits for them, and re-layouts  3.12 us (3%)
    ppermute x6, waiting for transfers between devices, local(): lax.ppermute(leaving, 'inst', [(i, i ^ 1 << bit) for i in range(N_INST)])  34.3 us
    ppermute x6, starting transfers between devices, local(): lax.ppermute(leaving, 'inst', [(i, i ^ 1 << bit) for i in range(N_INST)])  28.6 us
    all_to_all x1, starting transfers between devices, local(): lax.all_to_all(sent.reshape(N_INST * N_TP, MESSAGE // 4, 4, LANES), ('ins...  22.2 us
    pallas_call x1, Pallas kernels, prefill(): pl.pallas_call(prefill_kernel, out_shape=jax.ShapeDtypeStruct((SLOTS, GRO...  8.91 us
    pallas_call x1, Pallas kernels, dispatch(): pl.pallas_call(dispatch_kernel, out_shape=pltpu.HBM((rows, LANES), jnp.bf...  4.18 us
    unnamed x32, local copies, waits for them, and re-layouts  3.12 us
  transfers between devices with their start and end apart: 7, of which 1 were waited for; matrix products, arithmetic and copies ran while one was open for 0% of the time, Pallas kernels for 12%

profile of v5, /device:TPU:1, one launch (start us, length us, event | category | flops | bytes accessed | tf_op | source)
XLA Modules:
  0.0 107.7 jit_solution(11640814391410597430)
XLA Ops:
  0.6 4.2 %dispatch.1 = bf16[10240,128]{1,0:T(8,128)(2,1)} custom-call(s32[1]{0:T(128)} %bitcast.5.me_ref, s32[256,128]{1,0:T(8,128)} %bitcast.12, bf16[64,8192]{1,0:T(8,128)(2,1)} %queries_ref.1, bf16[512,256]{1,0:T(8,128)(2,1)} %bitcast.17), custom_call_target="tpu_custom_call" | custom-call | tf_op jit(solution)/shard_map/dispatch/pallas_call | solution.py:95
  4.8 0.0 copy-start.1
  4.8 0.0 copy-start.12
  4.8 0.0 copy-start.14
  4.9 0.0 copy-start.2
  4.9 0.0 copy-start.9
  4.9 0.0 copy-start.10
  4.9 22.2 %all-to-all-start = ((bf16[512,5,4,128]{3,2,1,0:T(4,128)(2,1)}), bf16[512,5,4,128]{3,2,1,0:T(4,128)(2,1)S(1)}, u32[]{:S(2)}, u32[]{:S(2)}) async-start(bf16[512,5,4,128]{3,2,1,0:T(4,128)(2,1)} %bitcast.16), calls=%async_computation | async-start | bytes 5242880 | tf_op jit(solution)/shard_map/all_to_all | solution.py:378
  27.1 0.0 copy-done.1
  27.1 0.0 copy-done.12
  27.1 0.0 copy-done.14
  27.1 0.0 copy-start
  27.1 1.2 %copy-done = bf16[128,16,1,256]{3,1,2,0:T(8,128)(2,1)S(1)} copy-done((bf16[128,16,1,256]{3,1,2,0:T(8,128)(2,1)S(1)}, bf16[128,16,1,256]{3,1,2,0:T(8,128)(2,1)}, u32[]{:S(2)}) %copy-start) | copy-done | bytes 1048600
  28.3 1.8 %prepare.1 = (bf16[256,256]{1,0:T(8,128)(2,1)}, bf16[2048,256]{1,0:T(8,128)(2,1)S(1)}, bf16[1024,128]{1,0:T(8,128)(2,1)S(1)}) custom-call(s32[1]{0:T(128)} %bitcast.inst_ref, s32[64]{0:T(128)S(1)} %copy-done.12, s32[8,16]{1,0:T(8,128)S(1)} %copy-done.14, bf16[2048,256]{1,0:T(8,128)(2,1)S(1)} %bitcast.11, s32[256,128]{1,0:T(8,128)S(1)} %bitcast.13), custom_call_target="tpu_custom_call" | custom-call | tf_op jit(solution)/shard_map/prepare/pallas_call | solution.py:146
  30.1 0.0 copy-done.2
  30.1 0.0 copy-done.9
  30.1 0.0 copy-done.10
  30.1 1.7 %decode.1 = (bf16[32,1024]{1,0:T(8,128)(2,1)S(1)}, bf16[64,128]{1,0:T(8,128)(2,1)S(1)}, f32[64,128]{1,0:T(8,128)S(1)}, bf16[128,128]{1,0:T(8,128)(2,1)S(1)}) custom-call(s32[1]{0:T(128)} %bitcast.inst_ref, s32[64]{0:T(128)S(1)} %copy-done.12, s32[512]{0:T(512)S(1)} %copy-done.10, bf16[32,1024]{1,0:T(8,128)(2,1)S(1)} %bitcast.14, ...), custom_call_target="tpu_custom_call" | custom-call | tf_op jit(solution)/shard_map/decode/pallas_call | solution.py:217
  31.9 0.6 copy-done.3
  32.5 0.6 copy-done.5
  33.1 0.6 copy-done.7
  33.7 3.3 %collective-permute-start = (bf16[256,256]{1,0:T(8,128)(2,1)}, bf16[256,256]{1,0:T(8,128)(2,1)S(1)}, u32[]{:S(2)}, u32[]{:S(2)}) collective-permute-start(bf16[256,256]{1,0:T(8,128)(2,1)} %get-tuple-element.22), channel_id=1, source_target_pairs={{0,8},{8,0},{16,24},{24,16},{32,40},{40,32},{48,56},{56,48},{64,72... | collective-permute-start | bytes 393224 | tf_op jit(solution)/shard_map/ppermute | solution.py:391
  37.0 4.0 %collective-permute-start.1 = (bf16[256,256]{1,0:T(8,128)(2,1)}, bf16[256,256]{1,0:T(8,128)(2,1)S(1)}, u32[]{:S(2)}, u32[]{:S(2)}) collective-permute-start(bf16[256,256]{1,0:T(8,128)(2,1)} %get-tuple-element.22), channel_id=1, source_target_pairs={{0,16},{8,24},{16,0},{24,8},{32,48},{40,56},{48,32},{56,40},{64,80... | collective-permute-start | bytes 393224 | tf_op jit(solution)/shard_map/ppermute | solution.py:391
  41.0 4.6 %collective-permute-start.2 = (bf16[256,256]{1,0:T(8,128)(2,1)}, bf16[256,256]{1,0:T(8,128)(2,1)S(1)}, u32[]{:S(2)}, u32[]{:S(2)}) collective-permute-start(bf16[256,256]{1,0:T(8,128)(2,1)} %get-tuple-element.22), channel_id=1, source_target_pairs={{0,32},{8,40},{16,48},{24,56},{32,0},{40,8},{48,16},{56,24},{64,96... | collective-permute-start | bytes 393224 | tf_op jit(solution)/shard_map/ppermute | solution.py:391
  45.6 3.1 %collective-permute-start.3 = (bf16[256,256]{1,0:T(8,128)(2,1)}, bf16[256,256]{1,0:T(8,128)(2,1)S(1)}, u32[]{:S(2)}, u32[]{:S(2)}) collective-permute-start(bf16[256,256]{1,0:T(8,128)(2,1)} %get-tuple-element.22), channel_id=1, source_target_pairs={{0,64},{8,72},{16,80},{24,88},{32,96},{40,104},{48,112},{56,120},{... | collective-permute-start | bytes 393224 | tf_op jit(solution)/shard_map/ppermute | solution.py:391
  48.7 4.3 %collective-permute-start.4 = (bf16[256,256]{1,0:T(8,128)(2,1)}, bf16[256,256]{1,0:T(8,128)(2,1)S(1)}, u32[]{:S(2)}, u32[]{:S(2)}) collective-permute-start(bf16[256,256]{1,0:T(8,128)(2,1)} %get-tuple-element.22), channel_id=1, source_target_pairs={{0,128},{8,136},{16,144},{24,152},{32,160},{40,168},{48,176},{56,1... | collective-permute-start | bytes 393224 | tf_op jit(solution)/shard_map/ppermute | solution.py:391
  53.1 34.3 %collective-permute-done.refs_0_ = bf16[256,256]{1,0:T(8,128)(2,1)S(1)} collective-permute-done((bf16[256,256]{1,0:T(8,128)(2,1)}, bf16[256,256]{1,0:T(8,128)(2,1)S(1)}, u32[]{:S(2)}, u32[]{:S(2)}) %collective-permute-start) | collective-permute-done | bytes 131104 | tf_op jit(solution)/shard_map/ppermute | solution.py:391
  87.3 9.2 %collective-permute-start.5 = (bf16[256,256]{1,0:T(8,128)(2,1)}, bf16[256,256]{1,0:T(8,128)(2,1)}, u32[]{:S(2)}, u32[]{:S(2)}) collective-permute-start(bf16[256,256]{1,0:T(8,128)(2,1)} %get-tuple-element.22), channel_id=1, source_target_pairs={{0,256},{8,264},{16,272},{24,280},{32,288},{40,296},{48,304},{56,3... | collective-permute-start | bytes 393224 | tf_op jit(solution)/shard_map/ppermute | solution.py:391
  96.6 0.0 all-to-all-done
  96.6 0.0 copy-start.4
  96.6 0.0 copy-start.6
  96.6 0.0 copy-start.8
  96.6 0.0 copy-start.11
  96.6 0.0 copy-start.13
  96.6 0.0 copy-start.15
  96.7 8.9 %prefill.1 = bf16[1024,1024]{1,0:T(8,128)(2,1)} custom-call(bf16[10240,128]{1,0:T(8,128)(2,1)S(1)} %bitcast.10, bf16[1024,128]{1,0:T(8,128)(2,1)S(1)} %get-tuple-element.15.mask_ref), custom_call_target="tpu_custom_call" | custom-call | tf_op jit(solution)/shard_map/prefill/pallas_call | solution.py:343
  105.6 0.0 collective-permute-done.1.refs_1_
  105.6 0.0 collective-permute-done.2.refs_2_
  105.6 0.0 collective-permute-done.3.refs_3_
  105.6 0.0 collective-permute-done.4.refs_4_
  105.6 0.0 collective-permute-done.5.refs_5_
  105.6 0.0 copy-done.4
  105.6 0.0 copy-done.6
  105.6 0.0 copy-done.8
  105.7 0.0 copy-done.11
  105.7 0.0 copy-done.13
  105.7 0.0 copy-done.15
  105.7 2.1 %traded.1 = bf16[32,1024]{1,0:T(8,128)(2,1)} custom-call(s32[1]{0:T(128)} %bitcast.inst_ref, s32[64]{0:T(128)S(1)} %copy-done.15, s32[64]{0:T(128)S(1)} %copy-done.13, s32[512]{0:T(512)S(1)} %copy-done.11, bf16[64,128]{1,0:T(8,128)(2,1)S(1)} %get-tuple-element.16.query_ref, f32[64,128]{1,0:T(8,128)S(1)} %copy-done.6, bf16[128,128]{1,0:T(8,128)(2,1)S(1)} %copy-done.8, ...), custom_call_target="tpu_custom_call" | custom-call | tf_op jit(solution)/shard_map/traded/pallas_call | solution.py:261
  (3 shorter events, 0.0 us)
Async XLA Ops:
  4.8 22.2 %copy-start.1 = (s32[32768,1]{0,1:T(1,128)S(1)}, s32[32768,1]{0,1:T(1,128)}, u32[]{:S(2)}) copy-start(s32[32768,1]{0,1:T(1,128)} %param.19) | copy-start | bytes 393220
  4.8 22.2 %copy-start.12 = (s32[64]{0:T(128)S(1)}, s32[64]{0:T(128)}, u32[]{:S(2)}) copy-start(s32[64]{0:T(128)} %slot_ref.5) | copy-start | bytes 772
  4.8 22.2 %copy-start.14 = (s32[8,16]{1,0:T(8,128)S(1)}, s32[8,16]{1,0:T(8,128)}, u32[]{:S(2)}) copy-start(s32[8,16]{1,0:T(8,128)} %table_ref.1) | copy-start | bytes 1540
  4.9 25.3 %copy-start.2 = (bf16[4,8,1024]{2,1,0:T(8,128)(2,1)S(1)}, bf16[4,8,1024]{2,1,0:T(8,128)(2,1)}, u32[]{:S(2)}) copy-start(bf16[4,8,1024]{2,1,0:T(8,128)(2,1)} %param.10) | copy-start | bytes 196612
  4.9 25.3 %copy-start.9 = (bf16[4,8,1,256]{3,1,2,0:T(8,128)(2,1)S(1)}, bf16[4,8,1,256]{3,1,2,0:T(8,128)(2,1)}, u32[]{:S(2)}) copy-start(bf16[4,8,1,256]{3,1,2,0:T(8,128)(2,1)} %param.11) | copy-start | bytes 49156
  4.9 25.2 %copy-start.10 = (s32[512]{0:T(512)S(1)}, s32[512]{0:T(512)}, u32[]{:S(2)}) copy-start(s32[512]{0:T(512)} %lens_ref.3) | copy-start | bytes 6148
  4.9 91.7 %all-to-all-start = ((bf16[512,5,4,128]{3,2,1,0:T(4,128)(2,1)}), bf16[512,5,4,128]{3,2,1,0:T(4,128)(2,1)S(1)}, u32[]{:S(2)}, u32[]{:S(2)}) async-start(bf16[512,5,4,128]{3,2,1,0:T(4,128)(2,1)} %bitcast.16), calls=%async_computation | async-start | bytes 5242880 | tf_op jit(solution)/shard_map/all_to_all | solution.py:378
  27.1 1.2 %copy-start = (bf16[128,16,1,256]{3,1,2,0:T(8,128)(2,1)S(1)}, bf16[128,16,1,256]{3,1,2,0:T(8,128)(2,1)}, u32[]{:S(2)}) copy-start(bf16[128,16,1,256]{3,1,2,0:T(8,128)(2,1)} %param.12) | copy-start | bytes 3145732
  31.9 0.6 copy-start.3
  32.5 0.6 copy-start.5
  33.1 0.6 copy-start.7
  33.7 53.6 %collective-permute-start = (bf16[256,256]{1,0:T(8,128)(2,1)}, bf16[256,256]{1,0:T(8,128)(2,1)S(1)}, u32[]{:S(2)}, u32[]{:S(2)}) collective-permute-start(bf16[256,256]{1,0:T(8,128)(2,1)} %get-tuple-element.22), channel_id=1, source_target_pairs={{0,8},{8,0},{16,24},{24,16},{32,40},{40,32},{48,56},{56,48},{64,72... | collective-permute-start | bytes 393224 | tf_op jit(solution)/shard_map/ppermute | solution.py:391
  37.0 68.6 %collective-permute-start.1 = (bf16[256,256]{1,0:T(8,128)(2,1)}, bf16[256,256]{1,0:T(8,128)(2,1)S(1)}, u32[]{:S(2)}, u32[]{:S(2)}) collective-permute-start(bf16[256,256]{1,0:T(8,128)(2,1)} %get-tuple-element.22), channel_id=1, source_target_pairs={{0,16},{8,24},{16,0},{24,8},{32,48},{40,56},{48,32},{56,40},{64,80... | collective-permute-start | bytes 393224 | tf_op jit(solution)/shard_map/ppermute | solution.py:391
  41.0 64.6 %collective-permute-start.2 = (bf16[256,256]{1,0:T(8,128)(2,1)}, bf16[256,256]{1,0:T(8,128)(2,1)S(1)}, u32[]{:S(2)}, u32[]{:S(2)}) collective-permute-start(bf16[256,256]{1,0:T(8,128)(2,1)} %get-tuple-element.22), channel_id=1, source_target_pairs={{0,32},{8,40},{16,48},{24,56},{32,0},{40,8},{48,16},{56,24},{64,96... | collective-permute-start | bytes 393224 | tf_op jit(solution)/shard_map/ppermute | solution.py:391
  45.6 60.0 %collective-permute-start.3 = (bf16[256,256]{1,0:T(8,128)(2,1)}, bf16[256,256]{1,0:T(8,128)(2,1)S(1)}, u32[]{:S(2)}, u32[]{:S(2)}) collective-permute-start(bf16[256,256]{1,0:T(8,128)(2,1)} %get-tuple-element.22), channel_id=1, source_target_pairs={{0,64},{8,72},{16,80},{24,88},{32,96},{40,104},{48,112},{56,120},{... | collective-permute-start | bytes 393224 | tf_op jit(solution)/shard_map/ppermute | solution.py:391
  48.7 56.9 %collective-permute-start.4 = (bf16[256,256]{1,0:T(8,128)(2,1)}, bf16[256,256]{1,0:T(8,128)(2,1)S(1)}, u32[]{:S(2)}, u32[]{:S(2)}) collective-permute-start(bf16[256,256]{1,0:T(8,128)(2,1)} %get-tuple-element.22), channel_id=1, source_target_pairs={{0,128},{8,136},{16,144},{24,152},{32,160},{40,168},{48,176},{56,1... | collective-permute-start | bytes 393224 | tf_op jit(solution)/shard_map/ppermute | solution.py:391
  87.3 18.3 %collective-permute-start.5 = (bf16[256,256]{1,0:T(8,128)(2,1)}, bf16[256,256]{1,0:T(8,128)(2,1)}, u32[]{:S(2)}, u32[]{:S(2)}) collective-permute-start(bf16[256,256]{1,0:T(8,128)(2,1)} %get-tuple-element.22), channel_id=1, source_target_pairs={{0,256},{8,264},{16,272},{24,280},{32,288},{40,296},{48,304},{56,3... | collective-permute-start | bytes 393224 | tf_op jit(solution)/shard_map/ppermute | solution.py:391
  96.6 9.0 %copy-start.4 = (bf16[32,1024]{1,0:T(8,128)(2,1)S(1)}, bf16[32,1024]{1,0:T(8,128)(2,1)}, u32[]{:S(2)}) copy-start(bf16[32,1024]{1,0:T(8,128)(2,1)} %copy-done.3) | copy-start | bytes 196612
  96.6 9.0 %copy-start.6 = (f32[64,128]{1,0:T(8,128)S(1)}, f32[64,128]{1,0:T(8,128)}, u32[]{:S(2)}) copy-start(f32[64,128]{1,0:T(8,128)} %copy-done.5) | copy-start | bytes 98308
  96.6 9.0 %copy-start.8 = (bf16[128,128]{1,0:T(8,128)(2,1)S(1)}, bf16[128,128]{1,0:T(8,128)(2,1)}, u32[]{:S(2)}) copy-start(bf16[128,128]{1,0:T(8,128)(2,1)} %copy-done.7) | copy-start | bytes 98308
  96.6 9.0 %copy-start.11 = (s32[512]{0:T(512)S(1)}, s32[512]{0:T(512)}, u32[]{:S(2)}) copy-start(s32[512]{0:T(512)} %lens_ref.3) | copy-start | bytes 6148
  96.6 9.0 %copy-start.13 = (s32[64]{0:T(128)S(1)}, s32[64]{0:T(128)}, u32[]{:S(2)}) copy-start(s32[64]{0:T(128)} %slot_ref.5) | copy-start | bytes 772
  96.6 9.0 %copy-start.15 = (s32[64]{0:T(128)S(1)}, s32[64]{0:T(128)}, u32[]{:S(2)}) copy-start(s32[64]{0:T(128)} %partner_ref.1) | copy-start | bytes 772
